TPU v7x, 128 devices: a whole 4x4x4 slice. The times are simulated.
128 devices in a mesh: freq: 4 (over z_lo, core), facet: 32 (over y, x, z_hi).
Axes of the slice: x: 4, y: 4, z: 4 (z_hi: 2, z_lo: 2; z = z_hi * 2 + z_lo), core: 2. Of those that a mesh axis runs over, the one named last changes fastest.
Arguments:
- visibilities: float32 [64, 2, 2048], P('facet', None, 'freq'), may hold values from -6 to 6
- weights: float32 [64, 2048], P('facet', 'freq'), may hold values from 0.1 to 1
- uv_cells: int32 [64, 2, 2048], P('facet', None, 'freq'), may hold values from -16384 to 16383
- flags: int32 [64, 2048], P('facet', 'freq'), may hold values from 0 to 1, as said below
- plan: int32 [64], replicated, may hold values from 0 to 63, each once
- beam: float32 [32, 64], P('facet'), may hold values from 0.2 to 1
- facets: int32 [32, 2], P('facet'), may hold values from 0 to 255
Outputs:
- dirty_image: float32 [32, 128, 128], P('facet', 'freq')
Inputs may be any that keep to these rules, and one draw needn't show every extreme that they name: `flags`: in each block, each frequency group's 512 rows hold at most 256 unflagged rows; in every draw some block holds exactly 256 in every group. `plan`: each of the 64 blocks is read at exactly one step.
All inputs are finite; a program needn't handle non-finite values.
Results may differ from a plain program's by a relative error of at most 0.0037.
Values sent between devices are 32-bit elements; how exact they have to be, the bound alone decides.
No kernel may reach another device: no remote copies, remote signals or barrier semaphores. Data moves between devices by JAX's collectives and lax.ppermute only.
A program may use at most 64 MiB of HBM per device.

v0:
```python
import math

import jax
import jax.numpy as jnp
from jax import lax
from jax.sharding import PartitionSpec as P

P_SIZE = 128
IMG = 32768


full_turn = 2.0 * math.pi
slab_limit = 16384
fine_count = 16


def angle_table(factors, cells):
    turns = jnp.mod(factors[:, None] * cells[None, :], IMG).astype(jnp.float32) * (full_turn / IMG)
    return (jnp.cos(turns), jnp.sin(turns))


def phase_table(base, cells):
    coarse_count = P_SIZE // fine_count
    base_cos, base_sin = angle_table(jnp.reshape(base, (1,)), cells)
    coarse_cos, coarse_sin = angle_table(
        jnp.arange(coarse_count, dtype=jnp.int32) * fine_count, cells
    )
    fine_cos, fine_sin = angle_table(jnp.arange(fine_count, dtype=jnp.int32), cells)
    outer_cos = base_cos * coarse_cos - base_sin * coarse_sin
    outer_sin = base_sin * coarse_cos + base_cos * coarse_sin
    full_cos = (
        outer_cos[:, None, :] * fine_cos[None, :, :] - outer_sin[:, None, :] * fine_sin[None, :, :]
    )
    full_sin = (
        outer_sin[:, None, :] * fine_cos[None, :, :] + outer_cos[:, None, :] * fine_sin[None, :, :]
    )
    extent = cells.shape[0]
    return (full_cos.reshape(P_SIZE, extent), full_sin.reshape(P_SIZE, extent))


def facet_image(samples, facet_col, facet_row):
    u_cells = samples[3].astype(jnp.int32)
    v_cells = samples[4].astype(jnp.int32)
    cos_u, sin_u = phase_table(facet_col * P_SIZE - IMG // 2, u_cells)
    real_part = samples[0] * samples[2]
    imag_part = samples[1] * samples[2]
    left = jnp.concatenate(
        [real_part * cos_u - imag_part * sin_u, -(real_part * sin_u + imag_part * cos_u)], axis=1
    ).astype(jnp.bfloat16)
    cos_v, sin_v = phase_table(facet_row * P_SIZE - IMG // 2, v_cells)
    right = jnp.concatenate([cos_v, sin_v], axis=1).astype(jnp.bfloat16)
    return lax.dot_general(
        left, right, (((1,), (1,)), ((), ())), preferred_element_type=jnp.float32
    )


def slab_image(samples, facet_col, facet_row):
    extent = samples.shape[1]
    slabs = samples.reshape(5, extent // slab_limit, slab_limit).transpose(1, 0, 2)

    def advance(running, slab):
        return (running + facet_image(slab, facet_col, facet_row), None)

    summed, _ = lax.scan(advance, jnp.zeros((P_SIZE, P_SIZE), jnp.float32), slabs)
    return summed


def flatten_blocks(packed, factors):
    scaled = packed[:, 2, :] * factors[:, None]
    joined = jnp.concatenate([packed[:, :2, :], scaled[:, None, :], packed[:, 3:, :]], axis=1)
    return joined.transpose(1, 0, 2).reshape(5, -1)


def body(visibilities, weights, uv_cells, flags, plan, beam, facets):
    live = weights * flags.astype(jnp.float32)
    packed = jnp.concatenate([visibilities, live[:, None, :], uv_cells.astype(jnp.float32)], axis=1)
    total_blocks = plan.shape[0]
    matches = (plan[:, None] == jnp.arange(total_blocks, dtype=jnp.int32)[None, :]).astype(
        jnp.float32
    )
    gains = jnp.sum(beam[0][:, None] * matches, axis=0)
    facet_col = facets[0, 0]
    facet_row = facets[0, 1]
    image = slab_image(
        flatten_blocks(lax.all_gather(packed, "facet", axis=0, tiled=True), gains),
        facet_col,
        facet_row,
    )
    share = lax.psum_scatter(image, "freq", scatter_dimension=0, tiled=True)
    scale = 2.0 / math.sqrt(total_blocks * weights.shape[1] * lax.axis_size("freq"))
    return (share * scale)[None]


def solution(mesh):
    in_specs = (
        P("facet", None, "freq"),
        P("facet", "freq"),
        P("facet", None, "freq"),
        P("facet", "freq"),
        P(),
        P("facet", None),
        P("facet", None),
    )
    out_specs = P("facet", "freq", None)
    return jax.shard_map(body, mesh=mesh, in_specs=in_specs, out_specs=out_specs, check_vma=False)
```

profile of v0, /device:TPU:0, one launch (start us, length us, event | category | flops | bytes accessed | tf_op | source)
XLA Modules:
  0.0 201.8 jit_solution(12933893324455298943)
XLA Ops:
  6.5 0.7 convert_multiply_fusion
  7.3 0.7 convert_element_type.174
  8.0 0.7 pad_maximum_fusion.1
  8.7 101.9 %all_gather.3 = f32[64,5,512]{2,1,0:T(8,128)S(1)} all-gather(f32[2,5,512]{2,1,0:T(8,128)S(1)} %pad_maximum_fusion.1), channel_id=1, replica_groups=mesh['freq'=4,'facet'=32] {'facet'}, dimensions={0}, use_global_device_ids=true | all-gather | bytes 675840 | tf_op jit(solution)/shard_map/all_gather | solution.py:85
  110.7 0.8 select_reduce_fusion
  111.7 1.3 fusion.55
  114.6 67.0 %while.14 = (s32[]{:T(128)}, f32[128,128]{1,0:T(8,128)S(1)}, f32[2,5,16384]{2,1,0:T(8,128)S(1)}, s32[]{:T(128)}, s32[]{:T(128)}, /*index=5*/s32[]{:T(128)}, s32[]{:T(128)}, s32[]{}, s32[]{}, s32[]{}, /*index=10*/s32[]{}) while((s32[]{:T(128)}, f32[128,128]{1,0:T(8,128)S(1)}, f32[2,5,16384]{2,1,0:T(8,128)S(1)}, s32[]{:T(128)}, ...), condition=%wide.region_2.3_spmd.clone, body=%wide.region_1.2_spmd.clone.sunk | while | flops 1168670720 | bytes 81461504 | solution.py:64
  115.5 4.3 %multiply_subtract_fusion.5 = (f32[8,16384]{1,0:T(8,128)S(1)}, f32[8,16384]{1,0:T(8,128)S(1)}, f32[8,16384]{1,0:T(8,128)S(1)}, f32[8,16384]{1,0:T(8,128)S(1)}) fusion(f32[16384]{0:T(1024)S(1)} %get-tuple-element.221, s32[16384]{0:T(1024)S(1)} %bitcast.58, s32[8]{0:T(128)S(1)} %iota_multiply_fusion.2, f32[16384]{0:T(1024)S(1)} %get-tuple-element.222, ...), kind=kLoop, calls=%fused_computation.62.clone.1 | loop fusion | flops 5242880 | bytes 2490400 | tf_op jit(solution)/shard_map/while/body/eval_jaxpr/sub | solution.py:29
  119.8 4.1 %fusion.67 = (f32[16,16384]{1,0:T(8,128)S(1)}, f32[16,16384]{1,0:T(8,128)S(1)}) fusion(s32[16384]{0:T(1024)S(1)} %bitcast.59), kind=kLoop, calls=%fused_computation.61.clone.1 | loop fusion | flops 3670016 | bytes 2162688 | tf_op jit(solution)/shard_map/while/body/eval_jaxpr/cos | solution.py:19
  123.9 2.3 %multiply_subtract_fusion.6 = (f32[8,16,16384]{2,1,0:T(8,128)S(1)}, f32[8,16,16384]{2,1,0:T(8,128)S(1)}) fusion(f32[16,16384]{1,0:T(8,128)S(1)} %get-tuple-element.230, f32[8,16384]{1,0:T(8,128)S(1)} %get-tuple-element.231, f32[16,16384]{1,0:T(8,128)S(1)} %get-tuple-element.232, f32[8,16384]{1,0:T(8,128)S(1)} %get-tuple-element.233), kind=kLoop, calls=%fused_computation.19.clone.1 | loop fusion | flops 12582912 | bytes 19922944 | tf_op jit(solution)/shard_map/while/body/eval_jaxpr/sub | solution.py:32
  126.2 5.4 %fusion.68 = (bf16[128,16384]{1,0:T(8,128)(2,1)}, bf16[128,16384]{1,0:T(8,128)(2,1)}) fusion(f32[8,16,16384]{2,1,0:T(8,128)S(1)} %get-tuple-element.234, f32[8,16,16384]{2,1,0:T(8,128)S(1)} %get-tuple-element.235, f32[16384]{0:T(1024)S(1)} %bitcast.62, f32[16384]{0:T(1024)S(1)} %bitcast.61), kind=kLoop, calls=%fused_computation.10.clone.1 | loop fusion | flops 18874368 | bytes 25296896 | tf_op jit(solution)/shard_map/convert.4
  131.7 4.1 %fusion.65 = (f32[16,16384]{1,0:T(8,128)S(1)}, f32[16,16384]{1,0:T(8,128)S(1)}) fusion(s32[16384]{0:T(1024)S(1)} %bitcast.56), kind=kLoop, calls=%fused_computation.59.clone.1 | loop fusion | flops 3670016 | bytes 2162688 | tf_op jit(solution)/shard_map/while/body/eval_jaxpr/cos | solution.py:19
  135.7 4.2 %subtract_convert_fusion.2 = (bf16[8,16,16384]{2,1,0:T(8,128)(2,1)}, bf16[8,16,16384]{2,1,0:T(8,128)(2,1)}) fusion(f32[16,16384]{1,0:T(8,128)S(1)} %get-tuple-element.219, f32[8,16384]{1,0:T(8,128)S(1)} %get-tuple-element.225, f32[16,16384]{1,0:T(8,128)S(1)} %get-tuple-element.226, f32[8,16384]{1,0:T(8,128)S(1)} %get-tuple-element.227), kind=kLoop, calls=%fused_computation.17.clone.1 | loop fusion | flops 16777216 | bytes 11534336 | tf_op jit(solution)/shard_map/convert.3
  139.9 8.2 %fusion.69 = f32[128,128]{1,0:T(8,128)S(1)} fusion(bf16[128,16384]{1,0:T(8,128)(2,1)} %bitcast.53, bf16[128,16384]{1,0:T(8,128)(2,1)} %bitcast.52, bf16[128,16384]{1,0:T(8,128)(2,1)} %get-tuple-element.238, bf16[128,16384]{1,0:T(8,128)(2,1)} %get-tuple-element.239, f32[128,128]{1,0:T(8,128)S(1)} %get-tuple-element.252, pred[]{:T(512)S(6)} %compare.15), kind=kOutput, calls=%fused_computation.48.clone.1 | convolution fusion | flops 1107329024 | bytes 16908288 | tf_op jit(solution)/shard_map/while/body/eval_jaxpr/dot_general | solution.py:52
  149.0 4.3 %multiply_subtract_fusion.5 = (f32[8,16384]{1,0:T(8,128)S(1)}, f32[8,16384]{1,0:T(8,128)S(1)}, f32[8,16384]{1,0:T(8,128)S(1)}, f32[8,16384]{1,0:T(8,128)S(1)}) fusion(f32[16384]{0:T(1024)S(1)} %get-tuple-element.221, s32[16384]{0:T(1024)S(1)} %bitcast.58, s32[8]{0:T(128)S(1)} %iota_multiply_fusion.2, f32[16384]{0:T(1024)S(1)} %get-tuple-element.222, ...), kind=kLoop, calls=%fused_computation.62.clone.1 | loop fusion | flops 5242880 | bytes 2490400 | tf_op jit(solution)/shard_map/while/body/eval_jaxpr/sub | solution.py:29
  153.3 4.1 %fusion.67 = (f32[16,16384]{1,0:T(8,128)S(1)}, f32[16,16384]{1,0:T(8,128)S(1)}) fusion(s32[16384]{0:T(1024)S(1)} %bitcast.59), kind=kLoop, calls=%fused_computation.61.clone.1 | loop fusion | flops 3670016 | bytes 2162688 | tf_op jit(solution)/shard_map/while/body/eval_jaxpr/cos | solution.py:19
  157.4 2.3 %multiply_subtract_fusion.6 = (f32[8,16,16384]{2,1,0:T(8,128)S(1)}, f32[8,16,16384]{2,1,0:T(8,128)S(1)}) fusion(f32[16,16384]{1,0:T(8,128)S(1)} %get-tuple-element.230, f32[8,16384]{1,0:T(8,128)S(1)} %get-tuple-element.231, f32[16,16384]{1,0:T(8,128)S(1)} %get-tuple-element.232, f32[8,16384]{1,0:T(8,128)S(1)} %get-tuple-element.233), kind=kLoop, calls=%fused_computation.19.clone.1 | loop fusion | flops 12582912 | bytes 19922944 | tf_op jit(solution)/shard_map/while/body/eval_jaxpr/sub | solution.py:32
  159.7 5.4 %fusion.68 = (bf16[128,16384]{1,0:T(8,128)(2,1)}, bf16[128,16384]{1,0:T(8,128)(2,1)}) fusion(f32[8,16,16384]{2,1,0:T(8,128)S(1)} %get-tuple-element.234, f32[8,16,16384]{2,1,0:T(8,128)S(1)} %get-tuple-element.235, f32[16384]{0:T(1024)S(1)} %bitcast.62, f32[16384]{0:T(1024)S(1)} %bitcast.61), kind=kLoop, calls=%fused_computation.10.clone.1 | loop fusion | flops 18874368 | bytes 25296896 | tf_op jit(solution)/shard_map/convert.4
  165.2 4.1 %fusion.65 = (f32[16,16384]{1,0:T(8,128)S(1)}, f32[16,16384]{1,0:T(8,128)S(1)}) fusion(s32[16384]{0:T(1024)S(1)} %bitcast.56), kind=kLoop, calls=%fused_computation.59.clone.1 | loop fusion | flops 3670016 | bytes 2162688 | tf_op jit(solution)/shard_map/while/body/eval_jaxpr/cos | solution.py:19
  169.2 4.2 %subtract_convert_fusion.2 = (bf16[8,16,16384]{2,1,0:T(8,128)(2,1)}, bf16[8,16,16384]{2,1,0:T(8,128)(2,1)}) fusion(f32[16,16384]{1,0:T(8,128)S(1)} %get-tuple-element.219, f32[8,16384]{1,0:T(8,128)S(1)} %get-tuple-element.225, f32[16,16384]{1,0:T(8,128)S(1)} %get-tuple-element.226, f32[8,16384]{1,0:T(8,128)S(1)} %get-tuple-element.227), kind=kLoop, calls=%fused_computation.17.clone.1 | loop fusion | flops 16777216 | bytes 11534336 | tf_op jit(solution)/shard_map/convert.3
  173.5 8.2 %fusion.69 = f32[128,128]{1,0:T(8,128)S(1)} fusion(bf16[128,16384]{1,0:T(8,128)(2,1)} %bitcast.53, bf16[128,16384]{1,0:T(8,128)(2,1)} %bitcast.52, bf16[128,16384]{1,0:T(8,128)(2,1)} %get-tuple-element.238, bf16[128,16384]{1,0:T(8,128)(2,1)} %get-tuple-element.239, f32[128,128]{1,0:T(8,128)S(1)} %get-tuple-element.252, pred[]{:T(512)S(6)} %compare.15), kind=kOutput, calls=%fused_computation.48.clone.1 | convolution fusion | flops 1107329024 | bytes 16908288 | tf_op jit(solution)/shard_map/while/body/eval_jaxpr/dot_general | solution.py:52
  181.7 0.6 copy-done
  182.3 11.3 %reduce-scatter.2.cloned.1.call-done = f32[32,128]{1,0:T(8,128)} async-done(((f32[128,128]{1,0:T(8,128)}), f32[32,128]{1,0:T(8,128)}) %reduce-scatter.2.cloned.1.call-update) | async-done | bytes 16400 | tf_op jit(solution)/shard_map/reduce_scatter | solution.py:89
  193.6 1.3 multiply_bitcast_fusion
  (14 shorter events, 2.3 us)
Async XLA Ops:
  6.5 187.1 %reduce-scatter.2.cloned.1.call-start = ((), (), s32[]{:S(2)}) async-start(), calls=%async_computation.1 | async-start | bytes 81920 | tf_op jit(solution)/shard_map/reduce_scatter | solution.py:89
  181.7 0.6 copy-start
Sparse Core Ops, SparseCore 0:
  182.5 11.0 reduce-scatter.1
where the time goes:
time: 203 us; the launch traced here: 202 us
  blocking collectives  102 us (50%)
  other arithmetic  55.2 us (27%)
  matrix products  16.4 us (8%)
  between operations  14.7 us (7%)
  waiting for transfers between devices  11.3 us (6%)
  local copies, waits for them, and re-layouts  2.13 us (1%)
    all_gather x1, blocking collectives, body(): lax.all_gather(packed, 'facet', axis=0, tiled=True)  102 us
    another operation x4, other arithmetic  19.3 us
    cos x6, other arithmetic, angle_table(): return (jnp.cos(turns), jnp.sin(turns))  17.3 us
    dot_general x2, matrix products, facet_image(): lax.dot_general(left, right, (((1,), (1,)), ((), ())), preferred_element_...  16.4 us
    reduce_scatter x1, waiting for transfers between devices, body(): share = lax.psum_scatter(image, 'freq', scatter_dimension=0, tiled=True)  11.3 us
    sub x2, other arithmetic, phase_table(): outer_cos = base_cos * coarse_cos - base_sin * coarse_sin  8.67 us
    sub x2, other arithmetic, phase_table(): outer_cos[:, None, :] * fine_cos[None, :, :]  4.64 us
  transfers between devices with their start and end apart: 1, of which 1 were waited for; matrix products, arithmetic and copies ran while one was open for 0% of the time, Pallas kernels for 0%

commit v1 on v0

v1 whole, which is shorter than its diff:
```python
import functools
import math

import jax
import jax.numpy as jnp
from jax import lax
from jax.experimental import pallas as pl
from jax.experimental.pallas import tpu as pltpu
from jax.sharding import PartitionSpec as P

P_SIZE = 128
IMG = 32768
KEEP = 256
LANES = 128
HALF = P_SIZE // 2


def lane_prefix(flags):
    rows = lax.broadcasted_iota(jnp.int32, (LANES, LANES), 0)
    columns = lax.broadcasted_iota(jnp.int32, (LANES, LANES), 1)
    earlier = (rows < columns).astype(jnp.bfloat16)
    running = jnp.zeros((flags.shape[0], 1), jnp.float32)
    parts = []
    for start in range(0, flags.shape[1], LANES):
        piece = flags[:, start : start + LANES]
        inside = jnp.dot(piece.astype(jnp.bfloat16), earlier, preferred_element_type=jnp.float32)
        parts.append(inside + running)
        running = running + jnp.sum(piece, axis=1, keepdims=True)
    return jnp.concatenate(parts, axis=1)


def pack_kernel(copies, vis_ref, weight_ref, uv_ref, flag_ref, out_ref, data_ref):
    rows = weight_ref.shape[1]
    flags = flag_ref[...].astype(jnp.float32)
    weights = weight_ref[...]
    data_ref[0:2, :] = vis_ref[:, 0, :] * weights
    data_ref[2:4, :] = vis_ref[:, 1, :] * weights
    data_ref[4:6, :] = uv_ref[:, 0, :].astype(jnp.float32)
    data_ref[6:8, :] = uv_ref[:, 1, :].astype(jnp.float32)
    data = data_ref[...]
    high = data.astype(jnp.bfloat16).astype(jnp.float32)
    rest = data - high
    middle = rest.astype(jnp.bfloat16).astype(jnp.float32)
    low = rest - middle
    pieces = jnp.concatenate([high, middle, low], axis=0).astype(jnp.bfloat16)
    spot = jnp.where(flags > 0.0, lane_prefix(flags), -1.0).astype(jnp.int32)
    target = lax.broadcasted_iota(jnp.int32, (KEEP, rows), 0)
    packed = []
    for block in range(2):
        chosen = (target == spot[block : block + 1, :]).astype(jnp.float32).astype(jnp.bfloat16)
        moved = lax.dot_general(
            pieces, chosen, (((1,), (1,)), ((), ())), preferred_element_type=jnp.float32
        )
        packed.append(moved[0:8] + moved[8:16] + moved[16:24])
    parity = lax.broadcasted_iota(jnp.int32, packed[0].shape, 0) & 1
    result = jnp.where(parity == 0, packed[0], packed[1])
    for copy in range(copies):
        out_ref[copy, 0:8, :] = result[:, :LANES]
        out_ref[copy, 8:16, :] = result[:, LANES:]


def sine_cosine(turns):
    quarter = (turns + 8192) >> 14
    x = (turns - (quarter << 14)).astype(jnp.float32) * (2.0 * math.pi / 65536.0)
    y = x * x
    sine = x * (1.0 + y * (-1.0 / 6 + y * (1.0 / 120 + y * (-1.0 / 5040 + y * (1.0 / 362880)))))
    cosine = 1.0 + y * (-0.5 + y * (1.0 / 24 + y * (-1.0 / 720 + y * (1.0 / 40320))))
    odd = (quarter & 1) == 1
    first = jnp.where(odd, cosine, sine)
    second = jnp.where(odd, sine, cosine)
    first = jnp.where((quarter & 2) == 2, -first, first)
    second = jnp.where(((quarter + 1) & 2) == 2, -second, second)
    return first, second


def half_steps(turns, count):
    sine, cosine = sine_cosine(turns)
    twice = 4.0 * cosine * cosine - 2.0
    sines, cosines = [sine], [cosine]
    before_sine, before_cosine = -sine, cosine
    for _ in range(count - 1):
        sines.append(twice * sines[-1] - before_sine)
        cosines.append(twice * cosines[-1] - before_cosine)
        before_sine, before_cosine = sines[-2], cosines[-2]
    return sines, cosines


def unfold(values, reverse):
    shape = values.shape
    lane = lax.broadcasted_iota(jnp.int32, shape, 1)
    source = jnp.where((lane & 8) == 8, lane, lane ^ 7)
    values = jnp.take_along_axis(values, source, axis=1)
    if reverse:
        values = jnp.take_along_axis(values, 7 - lax.broadcasted_iota(jnp.int32, shape, 0), axis=0)
    return values


def image_kernel(
    scale, facet_ref, plan_ref, beam_ref, data_ref, keep_ref, send_ref,
    fine_v, fine_u, outer, coarse, order_ref,
):
    owners = data_ref.shape[0] // 16
    column = 2 * (facet_ref[0, 0] * P_SIZE - IMG // 2) + (P_SIZE - 1)
    row = 2 * (facet_ref[0, 1] * P_SIZE - IMG // 2) + (P_SIZE - 1)

    def advance(step, sums):
        first = pl.multiple_of((step >> 1) * 128, 128)
        member = step & 1
        owner = lax.broadcasted_iota(jnp.int32, (8, plan_ref.shape[1]), 0) + (step >> 1) * 8
        gain = jnp.sum(
            jnp.where(plan_ref[...] == 2 * owner + member, beam_ref[...], 0.0),
            axis=1,
            keepdims=True,
        )
        even, odd = sums
        for start in range(0, KEEP, LANES):
            real, imag, u, v = (
                data_ref[pl.ds(first + start // 16 + 2 * kind + member, 8, stride=16), :]
                for kind in range(4)
            )
            u = u.astype(jnp.int32)
            v = v.astype(jnp.int32)
            real = real * gain
            imag = imag * gain
            sine, cosine = sine_cosine(u * column + v * row)
            centre_real = real * cosine - imag * sine
            centre_imag = real * sine + imag * cosine
            sines, cosines = half_steps(v, 8)
            for tau in range(8):
                fine_v[0, pl.ds(tau, 8, stride=8), :] = cosines[tau]
                fine_v[1, pl.ds(tau, 8, stride=8), :] = sines[tau]
            sines, cosines = half_steps(u, 8)
            for tau in range(8):
                fine_u[0, pl.ds(tau, 8, stride=8), :] = cosines[tau]
                fine_u[1, pl.ds(tau, 8, stride=8), :] = sines[tau]
            sines, cosines = half_steps(u << 4, 4)
            for far in range(4):
                coarse[2 * far] = cosines[far]
                coarse[2 * far + 1] = sines[far]
            sines, cosines = half_steps(v << 4, 4)
            for far in range(4):
                rc, isn = centre_real * cosines[far], centre_imag * sines[far]
                ic, rs = centre_imag * cosines[far], centre_real * sines[far]
                above, below = 4 + far, 3 - far
                outer[2 * above] = rc - isn
                outer[2 * above + 1] = ic + rs
                outer[2 * below] = rc + isn
                outer[2 * below + 1] = ic - rs
            for pair in range(4):
                table_a, table_b, table_c, table_s = [], [], [], []
                for chunk in (2 * pair, 2 * pair + 1):
                    rows = pl.ds(8 * chunk, 8)
                    cos_f, sin_f = fine_v[0, rows, :], fine_v[1, rows, :]
                    part_a, part_b, part_c, part_s = [], [], [], []
                    for far in range(8):
                        x = jnp.broadcast_to(outer[2 * far, pl.ds(chunk, 1), :], (8, LANES))
                        y = jnp.broadcast_to(outer[2 * far + 1, pl.ds(chunk, 1), :], (8, LANES))
                        xc, ys, yc, xs = x * cos_f, y * sin_f, y * cos_f, x * sin_f
                        part_a += [xc + ys, xc - ys]
                        part_b += [yc - xs, yc + xs]
                    cos_f, sin_f = fine_u[0, rows, :], fine_u[1, rows, :]
                    for far in range(4):
                        x = jnp.broadcast_to(coarse[2 * far, pl.ds(chunk, 1), :], (8, LANES))
                        y = jnp.broadcast_to(coarse[2 * far + 1, pl.ds(chunk, 1), :], (8, LANES))
                        xc, ys, yc, xs = x * cos_f, y * sin_f, y * cos_f, x * sin_f
                        part_c += [xc + ys, xc - ys]
                        part_s += [yc - xs, yc + xs]
                    for table, part in (
                        (table_a, part_a), (table_b, part_b), (table_c, part_c), (table_s, part_s)
                    ):
                        table.append(jnp.concatenate(part, axis=0).astype(jnp.bfloat16))
                a, b, c, s = (
                    jnp.concatenate(table, axis=1) for table in (table_a, table_b, table_c, table_s)
                )
                contract = (((1,), (1,)), ((), ()))
                even = even + lax.dot_general(c, a, contract, preferred_element_type=jnp.float32)
                odd = odd + lax.dot_general(s, b, contract, preferred_element_type=jnp.float32)
        return even, odd

    zero = jnp.zeros((HALF, P_SIZE), jnp.float32)
    even, odd = lax.fori_loop(0, owners // 4, advance, (zero, zero))
    upper = (even - odd) * scale
    lower = (even + odd) * scale
    core = lax.axis_index("freq") & 1
    far = lax.axis_index("freq") >> 1
    for index in range(16):
        piece = index // 4
        slot = ((piece & 1) ^ core) * 2 + ((piece >> 1) ^ far)
        if index >= 8:
            source = index - 8
            values = unfold(upper[8 * source : 8 * source + 8], source % 2 == 0)
        else:
            source = 7 - index
            values = unfold(lower[8 * source : 8 * source + 8], source % 2 == 1)
        place = pl.multiple_of(slot * 32 + 8 * (index % 4), 8)
        order_ref[pl.ds(place, 8), :] = values
    keep_ref[...] = order_ref[0:HALF, :]
    send_ref[...] = order_ref[HALF:, :]


VMEM = pl.BlockSpec(memory_space=pltpu.VMEM)
SMEM = pl.BlockSpec(memory_space=pltpu.SMEM)


def body(total, facet_devices, visibilities, weights, uv_cells, flags, plan, beam, facets):
    packed = pl.pallas_call(
        functools.partial(pack_kernel, facet_devices),
        out_shape=jax.ShapeDtypeStruct((facet_devices, 16, LANES), jnp.float32),
        in_specs=[VMEM] * 4,
        out_specs=VMEM,
        scratch_shapes=[pltpu.VMEM((8, weights.shape[1]), jnp.float32)],
    )(visibilities, weights, uv_cells, flags)
    gathered = lax.all_to_all(packed, "facet", 0, 0)
    image = jax.ShapeDtypeStruct((HALF, P_SIZE), jnp.float32)
    keep, send = pl.pallas_call(
        functools.partial(image_kernel, 2.0 / math.sqrt(total)),
        out_shape=(image, image),
        in_specs=[SMEM, VMEM, VMEM, VMEM],
        out_specs=(VMEM, VMEM),
        scratch_shapes=[
            pltpu.VMEM((2, 64, LANES), jnp.float32),
            pltpu.VMEM((2, 64, LANES), jnp.float32),
            pltpu.VMEM((16, 8, LANES), jnp.float32),
            pltpu.VMEM((8, 8, LANES), jnp.float32),
            pltpu.VMEM((P_SIZE, P_SIZE), jnp.float32),
        ],
    )(facets, plan[None], beam, gathered.reshape(facet_devices * 16, LANES))
    half = keep + lax.ppermute(send, "freq", [(i, i ^ 1) for i in range(4)])
    return (half[:32] + lax.ppermute(half[32:], "freq", [(i, i ^ 2) for i in range(4)]))[None]


def solution(mesh):
    in_specs = (
        P("facet", None, "freq"),
        P("facet", "freq"),
        P("facet", None, "freq"),
        P("facet", "freq"),
        P(),
        P("facet", None),
        P("facet", None),
    )
    total = 64 * 2048
    return jax.shard_map(
        functools.partial(body, total, mesh.shape["facet"]),
        mesh=mesh,
        in_specs=in_specs,
        out_specs=P("facet", "freq", None),
        check_vma=False,
    )
```

time: 203 us -> 36.8 us (0.18)
  blocking collectives: 102 us -> 21.8 us
  other arithmetic: 55.2 us -> 1.37 us
  matrix products: 16.4 us -> 0 us
  between operations: 14.7 us -> 0.01 us
  Pallas kernels: 0 us -> 8.15 us
  waiting for transfers between devices: 11.3 us -> 4.13 us
  local copies, waits for them, and re-layouts: 2.13 us -> 0.01 us
    all_gather x1 -> x0, blocking collectives: 102 us -> none  [body(): lax.all_gather(packed, 'facet', axis=0, tiled=True)]
    all_to_all x0 -> x1, blocking collectives: none -> 21.8 us  [body(): gathered = lax.all_to_all(packed, 'facet', 0, 0)]
    another operation x4 -> x0, other arithmetic: 19.3 us -> none
    cos x6 -> x0, other arithmetic: 17.3 us -> none  [angle_table(): return (jnp.cos(turns), jnp.sin(turns))]
    dot_general x2 -> x0, matrix products: 16.4 us -> none  [facet_image(): lax.dot_general(left, right, (((1,), (1,)), ((), ())), preferred_element_...]
    sub x4 -> x0, other arithmetic: 13.3 us -> none  [the longest x2 8.67 us: phase_table(): outer_cos = base_cos * coarse_cos - base_sin * coarse_sin]
    reduce_scatter x1 -> x0, waiting for transfers between devices: 11.3 us -> none  [body(): share = lax.psum_scatter(image, 'freq', scatter_dimension=0, tiled=True)]
    pallas_call x0 -> x2, Pallas kernels: none -> 8.15 us  [the longest x1 6.25 us: body(): pl.pallas_call(functools.partial(image_kernel, 2.0 / math.sqrt(total)), o...]
  transfers between devices with their start and end apart: 1 -> 2, of which waited for: 1 -> 2; matrix products, arithmetic and copies ran while one was open for 0% -> 0% of each run, Pallas kernels for 0% -> 0%
where the time goes in v1:
time: 36.8 us; the launch traced here: 36.5 us
  blocking collectives  21.8 us (59%)
  Pallas kernels  8.15 us (22%)
  waiting for transfers between devices  4.13 us (11%)
  other arithmetic  1.37 us (4%)
  starting transfers between devices  1.02 us (3%)
    all_to_all x1, blocking collectives, body(): gathered = lax.all_to_all(packed, 'facet', 0, 0)  21.8 us
    pallas_call x1, Pallas kernels, body(): pl.pallas_call(functools.partial(image_kernel, 2.0 / math.sqrt(total)), o...  6.25 us
    ppermute x1, waiting for transfers between devices, body(): lax.ppermute(half[32:], 'freq', [(i, i ^ 2) for i in range(4)])  2.72 us
    pallas_call x1, Pallas kernels, body(): pl.pallas_call(functools.partial(pack_kernel, facet_devices), out_shape=j...  1.9 us
    ppermute x1, waiting for transfers between devices, body(): half = keep + lax.ppermute(send, 'freq', [(i, i ^ 1) for i in range(4)])  1.42 us
    ppermute x1, starting transfers between devices, body(): lax.ppermute(half[32:], 'freq', [(i, i ^ 2) for i in range(4)])  1.02 us
    add x1, other arithmetic, body(): half = keep + lax.ppermute(send, 'freq', [(i, i ^ 1) for i in range(4)])  0.77 us
  transfers between devices with their start and end apart: 2, of which 2 were waited for; matrix products, arithmetic and copies ran while one was open for 0% of the time, Pallas kernels for 0%

profile of v1, /device:TPU:0, one launch (start us, length us, event | category | flops | bytes accessed | tf_op | source)
XLA Modules:
  0.0 36.5 jit_solution(15571342498862344901)
XLA Ops:
  0.0 1.9 %shard_map.73 = f32[32,16,128]{2,1,0:T(8,128)} custom-call(f32[2,2,512]{2,1,0:T(2,128)} %vis_ref.1, f32[2,512]{1,0:T(2,128)} %weight_ref.1, s32[2,2,512]{2,1,0:T(2,128)} %uv_ref.1, s32[2,512]{1,0:T(2,128)} %flag_ref.1), custom_call_target="tpu_custom_call" | custom-call | tf_op jit(solution)/shard_map/pallas_call | solution.py:206
  1.9 21.8 %all_to_all.5 = f32[32,16,128]{2,1,0:T(8,128)} all-to-all(f32[32,16,128]{2,1,0:T(8,128)} %shard_map.73), channel_id=1, replica_groups=mesh['freq'=4,'facet'=32] {'facet'}, dimensions={0} | all-to-all | bytes 524288 | tf_op jit(solution)/shard_map/all_to_all | solution.py:213
  23.7 6.2 %shard_map.74 = (f32[64,128]{1,0:T(8,128)}, f32[64,128]{1,0:T(8,128)}) custom-call(s32[1,2]{1,0:T(1,128)} %facet_ref.1, s32[1,64]{1,0:T(1,128)} %bitcast.5, f32[1,64]{1,0:T(1,128)} %beam_ref.1, f32[512,128]{1,0:T(8,128)} %bitcast.4), custom_call_target="tpu_custom_call" | custom-call | tf_op jit(solution)/shard_map/pallas_call | solution.py:215
  29.9 0.0 collective-permute-start
  29.9 1.4 %collective-permute-done = f32[64,128]{1,0:T(8,128)S(1)} collective-permute-done((f32[64,128]{1,0:T(8,128)}, f32[64,128]{1,0:T(8,128)S(1)}, u32[]{:S(2)}, u32[]{:S(2)}) %collective-permute-start) | collective-permute-done | bytes 32800 | tf_op jit(solution)/shard_map/ppermute | solution.py:228
  31.3 0.8 %add.6 = f32[64,128]{1,0:T(8,128)S(1)} add(f32[64,128]{1,0:T(8,128)} %get-tuple-element.7, f32[64,128]{1,0:T(8,128)S(1)} %collective-permute-done) | non-fusion elementwise | flops 8192 | bytes 98304 | tf_op jit(solution)/shard_map/add | solution.py:228
  32.1 1.0 %collective-permute-start.1 = (f32[32,128]{1,0:T(8,128)S(1)}, f32[32,128]{1,0:T(8,128)S(1)}, u32[]{:S(2)}, u32[]{:S(2)}) collective-permute-start(f32[32,128]{1,0:T(8,128)S(1)} %slice.9), channel_id=1, source_target_pairs={{0,64},{32,96},{64,0},{96,32},{1,65},{33,97},{65,1},{97,33},{2,66}... | collective-permute-start | bytes 49160 | tf_op jit(solution)/shard_map/ppermute | solution.py:229
  33.1 2.7 %collective-permute-done.1 = f32[32,128]{1,0:T(8,128)S(1)} collective-permute-done((f32[32,128]{1,0:T(8,128)S(1)}, f32[32,128]{1,0:T(8,128)S(1)}, u32[]{:S(2)}, u32[]{:S(2)}) %collective-permute-start.1) | collective-permute-done | bytes 16416 | tf_op jit(solution)/shard_map/ppermute | solution.py:229
  35.9 0.6 %fusion = f32[1,32,128]{2,1,0:T(8,128)} fusion(f32[32,128]{1,0:T(8,128)S(1)} %collective-permute-done.1, f32[64,128]{1,0:T(8,128)S(1)} %add.6), kind=kLoop, calls=%fused_computation.1 | loop fusion | flops 4096 | bytes 49152 | tf_op jit(solution)/shard_map/broadcast_in_dim | solution.py:229
  (1 shorter events, 0.0 us)
Async XLA Ops:
  29.9 1.4 %collective-permute-start = (f32[64,128]{1,0:T(8,128)}, f32[64,128]{1,0:T(8,128)S(1)}, u32[]{:S(2)}, u32[]{:S(2)}) collective-permute-start(f32[64,128]{1,0:T(8,128)} %get-tuple-element.8), channel_id=1, source_target_pairs={{0,32},{32,0},{64,96},{96,64},{1,33},{33,1},{65,97},{97,65},{2,34}... | collective-permute-start | bytes 98312 | tf_op jit(solution)/shard_map/ppermute | solution.py:228
  32.1 3.7 %collective-permute-start.1 = (f32[32,128]{1,0:T(8,128)S(1)}, f32[32,128]{1,0:T(8,128)S(1)}, u32[]{:S(2)}, u32[]{:S(2)}) collective-permute-start(f32[32,128]{1,0:T(8,128)S(1)} %slice.9), channel_id=1, source_target_pairs={{0,64},{32,96},{64,0},{96,32},{1,65},{33,97},{65,1},{97,33},{2,66}... | collective-permute-start | bytes 49160 | tf_op jit(solution)/shard_map/ppermute | solution.py:229

commit v2 on v1

v2 whole, which is shorter than its diff:
```python
import functools
import math

import jax
import jax.numpy as jnp
from jax import lax
from jax.experimental import pallas as pl
from jax.experimental.pallas import tpu as pltpu
from jax.sharding import PartitionSpec as P

P_SIZE = 128
IMG = 32768
KEEP = 256
LANES = 128
HALF = P_SIZE // 2


def lane_prefix(flags):
    rows = lax.broadcasted_iota(jnp.int32, (LANES, LANES), 0)
    columns = lax.broadcasted_iota(jnp.int32, (LANES, LANES), 1)
    earlier = (rows < columns).astype(jnp.bfloat16)
    running = jnp.zeros((flags.shape[0], 1), jnp.float32)
    parts = []
    for start in range(0, flags.shape[1], LANES):
        piece = flags[:, start : start + LANES]
        inside = jnp.dot(piece.astype(jnp.bfloat16), earlier, preferred_element_type=jnp.float32)
        parts.append(inside + running)
        running = running + jnp.sum(piece, axis=1, keepdims=True)
    return jnp.concatenate(parts, axis=1)


def pack_kernel(copies, vis_ref, weight_ref, uv_ref, flag_ref, out_ref, data_ref):
    rows = weight_ref.shape[1]
    flags = flag_ref[...].astype(jnp.float32)
    weights = weight_ref[...]
    data_ref[0:2, :] = vis_ref[:, 0, :] * weights
    data_ref[2:4, :] = vis_ref[:, 1, :] * weights
    data_ref[4:6, :] = uv_ref[:, 0, :].astype(jnp.float32)
    data_ref[6:8, :] = uv_ref[:, 1, :].astype(jnp.float32)
    data = data_ref[...]
    high = data.astype(jnp.bfloat16).astype(jnp.float32)
    rest = data - high
    middle = rest.astype(jnp.bfloat16).astype(jnp.float32)
    low = rest - middle
    pieces = jnp.concatenate([high, middle, low], axis=0).astype(jnp.bfloat16)
    spot = jnp.where(flags > 0.0, lane_prefix(flags), -1.0).astype(jnp.int32)
    target = lax.broadcasted_iota(jnp.int32, (KEEP, rows), 0)
    packed = []
    for block in range(2):
        chosen = (target == spot[block : block + 1, :]).astype(jnp.float32).astype(jnp.bfloat16)
        moved = lax.dot_general(
            pieces, chosen, (((1,), (1,)), ((), ())), preferred_element_type=jnp.float32
        )
        packed.append(moved[0:8] + moved[8:16] + moved[16:24])
    parity = lax.broadcasted_iota(jnp.int32, packed[0].shape, 0) & 1
    result = jnp.where(parity == 0, packed[0], packed[1])
    for copy in range(copies):
        out_ref[copy, 0:8, :] = result[:, :LANES]
        out_ref[copy, 8:16, :] = result[:, LANES:]


def doubled(sine, cosine):
    twice = sine + sine
    return twice * cosine, 1.0 - twice * sine


def sine_cosine(turns):
    x = ((turns << 16) >> 16).astype(jnp.float32) * (2.0 * math.pi / 65536.0 / 4.0)
    y = x * x
    sine = x * (1.0 + y * (-1.0 / 6 + y * (1.0 / 120 + y * (-1.0 / 5040 + y * (1.0 / 362880)))))
    cosine = 1.0 + y * (-0.5 + y * (1.0 / 24 + y * (-1.0 / 720 + y * (1.0 / 40320))))
    return doubled(*doubled(sine, cosine))


def half_steps(sine, cosine, count):
    twice = 4.0 * cosine * cosine - 2.0
    sines, cosines = [sine], [cosine]
    before_sine, before_cosine = -sine, cosine
    for _ in range(count - 1):
        sines.append(twice * sines[-1] - before_sine)
        cosines.append(twice * cosines[-1] - before_cosine)
        before_sine, before_cosine = sines[-2], cosines[-2]
    return sines, cosines


def chunk_tables(outer, fine, count, chunk):
    cosine, sine = fine[0, pl.ds(8 * chunk, 8), :], fine[1, pl.ds(8 * chunk, 8), :]
    first, second = [], []
    for far in range(count):
        x = jnp.broadcast_to(outer[2 * far, pl.ds(chunk, 1), :], (8, LANES))
        y = jnp.broadcast_to(outer[2 * far + 1, pl.ds(chunk, 1), :], (8, LANES))
        first += [x * cosine, y * sine]
        second += [y * cosine, x * sine]
    return (
        jnp.concatenate(first, axis=0).astype(jnp.bfloat16),
        jnp.concatenate(second, axis=0).astype(jnp.bfloat16),
    )


def prepare(centre, data_ref, gain_ref, step, half, buffers):
    fine_v, fine_u, outer, coarse = buffers
    column, row = centre
    tile = step >> 1
    member = step & 1
    gain = gain_ref[pl.ds(pl.multiple_of(member * (gain_ref.shape[0] // 2) + tile * 8, 8), 8), :]
    first = tile * 128 + 8 * half + member
    real, imag, u, v = (
        data_ref[pl.ds(first + 2 * kind, 8, stride=16), :] for kind in range(4)
    )
    u = u.astype(jnp.int32)
    v = v.astype(jnp.int32)
    real = real * gain
    imag = imag * gain
    sine, cosine = sine_cosine(u * column + v * row)
    centre_real = real * cosine - imag * sine
    centre_imag = real * sine + imag * cosine
    near_v = sine_cosine(v)
    near_u = sine_cosine(u)
    for near, fine in ((near_v, fine_v), (near_u, fine_u)):
        sines, cosines = half_steps(*near, 8)
        for tau in range(8):
            fine[0, pl.ds(tau, 8, stride=8), :] = cosines[tau]
            fine[1, pl.ds(tau, 8, stride=8), :] = sines[tau]
    for _ in range(4):
        near_v = doubled(*near_v)
        near_u = doubled(*near_u)
    sines, cosines = half_steps(*near_u, 4)
    for far in range(4):
        coarse[2 * far] = cosines[far]
        coarse[2 * far + 1] = sines[far]
    sines, cosines = half_steps(*near_v, 4)
    for far in range(4):
        rc, isn = centre_real * cosines[far], centre_imag * sines[far]
        ic, rs = centre_imag * cosines[far], centre_real * sines[far]
        above, below = 4 + far, 3 - far
        outer[2 * above] = rc - isn
        outer[2 * above + 1] = ic + rs
        outer[2 * below] = rc + isn
        outer[2 * below + 1] = ic - rs


def accumulate(buffers, sums):
    fine_v, fine_u, outer, coarse = buffers
    even, odd = sums
    for pair in range(4):
        tables = [
            chunk_tables(coarse, fine_u, 4, chunk) + chunk_tables(outer, fine_v, 8, chunk)
            for chunk in (2 * pair, 2 * pair + 1)
        ]
        c, s, a, b = (jnp.concatenate(table, axis=1) for table in zip(*tables))
        contract = (((1,), (1,)), ((), ()))
        even = even + lax.dot_general(c, a, contract, preferred_element_type=jnp.float32)
        odd = odd + lax.dot_general(s, b, contract, preferred_element_type=jnp.float32)
    return even, odd


def paired(values, source, reverse):
    values = jnp.take_along_axis(values, source, axis=1)
    if reverse:
        values = jnp.take_along_axis(
            values, 7 - lax.broadcasted_iota(jnp.int32, values.shape, 0), axis=0
        )
    return values


def sum_blocks(block_of, facet_ref, plan_ref, beam_ref, data_ref, scratch, sums):
    gain_ref, buffers = scratch[0], (scratch[1:5], scratch[5:9])
    owners = data_ref.shape[0] // 16
    centre = tuple(2 * (facet_ref[0, k] * P_SIZE - IMG // 2) + (P_SIZE - 1) for k in range(2))
    for member in range(2):
        owner = lax.broadcasted_iota(jnp.int32, (owners, plan_ref.shape[1]), 0)
        matches = plan_ref[...] == block_of(owner, member)
        gain = jnp.sum(jnp.where(matches, beam_ref[...], 0.0), axis=1, keepdims=True)
        gain_ref[member * owners : (member + 1) * owners, :] = jnp.broadcast_to(
            gain, (owners, LANES)
        )
    steps = owners // 4
    prepare(centre, data_ref, gain_ref, 0, 0, buffers[0])

    def advance(step, sums):
        prepare(centre, data_ref, gain_ref, step, 1, buffers[1])
        sums = accumulate(buffers[0], sums)
        prepare(centre, data_ref, gain_ref, (step + 1) & (steps - 1), 0, buffers[0])
        return accumulate(buffers[1], sums)

    return lax.fori_loop(0, steps, advance, sums)


def first_kernel(facet_ref, plan_ref, beam_ref, data_ref, even_ref, odd_ref, *scratch):
    side = lax.axis_index("facet") & 1
    zero = jnp.zeros((HALF, P_SIZE), jnp.float32)
    even, odd = sum_blocks(
        lambda owner, member: 4 * owner + 2 * side + member,
        facet_ref, plan_ref, beam_ref, data_ref, scratch, (zero, zero),
    )
    even_ref[...] = even
    odd_ref[...] = odd


def last_kernel(
    scale, facet_ref, plan_ref, beam_ref, data_ref, even_ref, odd_ref, keep_ref, send_ref,
    order_ref, *scratch,
):
    side = 1 - (lax.axis_index("facet") & 1)
    even, odd = sum_blocks(
        lambda owner, member: 4 * owner + 2 * side + member,
        facet_ref, plan_ref, beam_ref, data_ref, scratch, (even_ref[...], odd_ref[...]),
    )
    even, odd = even * scale, odd * scale
    core = lax.axis_index("freq") & 1
    far = lax.axis_index("freq") >> 1
    lane = lax.broadcasted_iota(jnp.int32, (8, P_SIZE), 1)
    near = jnp.where((lane & 8) == 8, lane ^ 8, lane ^ 7)
    sign = jnp.where((lane & 8) == 8, -1.0, 1.0)
    for block in range(8):
        base = 16 * (block // 2)
        above = block % 2 == 1
        even_p, even_q = even[base : base + 8], even[base + 8 : base + 16]
        odd_p, odd_q = odd[base : base + 8], odd[base + 8 : base + 16]
        even_row = even_p - even_q if above else even_p + even_q
        odd_row = odd_p + odd_q if above else odd_p - odd_q
        less, more = even_row - odd_row, even_row + odd_row
        for index, one, two, reverse in (
            (8 + block, less, more, not above),
            (7 - block, more, less, above),
        ):
            values = paired(one, near, reverse) + sign * paired(two, near ^ 8, reverse)
            piece = index // 4
            slot = ((piece & 1) ^ core) * 2 + ((piece >> 1) ^ far)
            place = pl.multiple_of(slot * 32 + 8 * (index % 4), 8)
            order_ref[pl.ds(place, 8), :] = values
    keep_ref[...] = order_ref[0:HALF, :]
    send_ref[...] = order_ref[HALF:, :]


SMALL = pltpu.CompilerParams(vmem_limit_bytes=8 << 20)
VMEM = pl.BlockSpec(memory_space=pltpu.VMEM)
SMEM = pl.BlockSpec(memory_space=pltpu.SMEM)


def body(total, plane, visibilities, weights, uv_cells, flags, plan, beam, facets):
    packed = pl.pallas_call(
        functools.partial(pack_kernel, plane),
        out_shape=jax.ShapeDtypeStruct((plane, 16, LANES), jnp.float32),
        in_specs=[VMEM] * 4,
        out_specs=VMEM,
        scratch_shapes=[pltpu.VMEM((8, weights.shape[1]), jnp.float32)],
        compiler_params=SMALL,
    )(visibilities, weights, uv_cells, flags)
    groups = [list(range(side, 2 * plane, 2)) for side in range(2)]
    near = lax.all_to_all(packed, "facet", 0, 0, axis_index_groups=groups)
    near = near.reshape(plane * 16, LANES)
    far = lax.ppermute(near, "facet", [(i, i ^ 1) for i in range(2 * plane)])
    image = jax.ShapeDtypeStruct((HALF, P_SIZE), jnp.float32)
    buffers = [
        pltpu.VMEM((2, 64, LANES), jnp.float32),
        pltpu.VMEM((2, 64, LANES), jnp.float32),
        pltpu.VMEM((16, 8, LANES), jnp.float32),
        pltpu.VMEM((8, 8, LANES), jnp.float32),
    ]
    scratch = [pltpu.VMEM((2 * plane, LANES), jnp.float32)] + buffers * 2
    cost = pl.CostEstimate(
        flops=2 * 2 * HALF * P_SIZE * 2 * plane * KEEP, bytes_accessed=1 << 18, transcendentals=0
    )
    even, odd = pl.pallas_call(
        first_kernel,
        out_shape=(image, image),
        in_specs=[SMEM, VMEM, VMEM, VMEM],
        out_specs=(VMEM, VMEM),
        scratch_shapes=scratch,
        compiler_params=SMALL,
        cost_estimate=cost,
    )(facets, plan[None], beam, near)
    keep, send = pl.pallas_call(
        functools.partial(last_kernel, 2.0 / math.sqrt(total)),
        out_shape=(image, image),
        in_specs=[SMEM, VMEM, VMEM, VMEM, VMEM, VMEM],
        out_specs=(VMEM, VMEM),
        scratch_shapes=[pltpu.VMEM((P_SIZE, P_SIZE), jnp.float32)] + scratch,
        compiler_params=SMALL,
        cost_estimate=cost,
    )(facets, plan[None], beam, far, even, odd)
    half = keep + lax.ppermute(send, "freq", [(i, i ^ 1) for i in range(4)])
    return (half[:32] + lax.ppermute(half[32:], "freq", [(i, i ^ 2) for i in range(4)]))[None]


def solution(mesh):
    in_specs = (
        P("facet", None, "freq"),
        P("facet", "freq"),
        P("facet", None, "freq"),
        P("facet", "freq"),
        P(),
        P("facet", None),
        P("facet", None),
    )
    total = 64 * 2048
    return jax.shard_map(
        functools.partial(body, total, mesh.shape["facet"] // 2),
        mesh=mesh,
        in_specs=in_specs,
        out_specs=P("facet", "freq", None),
        check_vma=False,
    )
```

time: 36.8 us -> 33.9 us (0.921)
  blocking collectives: 21.8 us -> 14.9 us
  starting transfers between devices: 1.02 us -> 5.61 us
  local copies, waits for them, and re-layouts: 0.01 us -> 2.78 us
  Pallas kernels: 8.15 us -> 6.17 us
  other arithmetic: 1.37 us -> 0.61 us
  waiting for transfers between devices: 4.13 us -> 3.5 us
    all_to_all x1, blocking collectives: 21.8 us -> 14.9 us  [body(): near = lax.all_to_all(packed, 'facet', 0, 0, axis_index_groups=groups)]
    ppermute x0 -> x1, starting transfers between devices: none -> 3.88 us  [body(): far = lax.ppermute(near, 'facet', [(i, i ^ 1) for i in range(2 * plane)])]
    unnamed x0 -> x14, local copies, waits for them, and re-layouts: none -> 2.78 us
    pallas_call x2 -> x3, Pallas kernels: 8.15 us -> 6.17 us  [the longest x1 2.93 us: body(): pl.pallas_call(functools.partial(last_kernel, 2.0 / math.sqrt(total)), ou...]
    add x1, other arithmetic: 0.77 us -> 0.01 us  [body(): half = keep + lax.ppermute(send, 'freq', [(i, i ^ 1) for i in range(4)])]
    ppermute x1, starting transfers between devices: 1.02 us -> 1.65 us  [body(): lax.ppermute(half[32:], 'freq', [(i, i ^ 2) for i in range(4)])]
    ppermute x1, waiting for transfers between devices: 2.72 us -> 2.17 us  [body(): lax.ppermute(half[32:], 'freq', [(i, i ^ 2) for i in range(4)])]
  transfers between devices with their start and end apart: 2 -> 3, of which waited for: 2 -> 3; matrix products, arithmetic and copies ran while one was open for 0% -> 0% of each run, Pallas kernels for 0% -> 8%
where the time goes in v2:
time: 33.9 us; the launch traced here: 33.7 us
  blocking collectives  14.9 us (44%)
  Pallas kernels  6.17 us (18%)
  starting transfers between devices  5.61 us (17%)
  waiting for transfers between devices  3.5 us (10%)
  local copies, waits for them, and re-layouts  2.78 us (8%)
  other arithmetic  0.61 us (2%)
    all_to_all x1, blocking collectives, body(): near = lax.all_to_all(packed, 'facet', 0, 0, axis_index_groups=groups)  14.9 us
    ppermute x1, starting transfers between devices, body(): far = lax.ppermute(near, 'facet', [(i, i ^ 1) for i in range(2 * plane)])  3.88 us
    pallas_call x1, Pallas kernels, body(): pl.pallas_call(functools.partial(last_kernel, 2.0 / math.sqrt(total)), ou...  2.93 us
    pallas_call x1, Pallas kernels, body(): pl.pallas_call(first_kernel, out_shape=(image, image), in_specs=[SMEM, VM...  2.79 us
    unnamed x14, local copies, waits for them, and re-layouts  2.78 us
    ppermute x1, waiting for transfers between devices, body(): lax.ppermute(half[32:], 'freq', [(i, i ^ 2) for i in range(4)])  2.17 us
    ppermute x1, starting transfers between devices, body(): lax.ppermute(half[32:], 'freq', [(i, i ^ 2) for i in range(4)])  1.65 us
    ppermute x1, waiting for transfers between devices, body(): half = keep + lax.ppermute(send, 'freq', [(i, i ^ 1) for i in range(4)])  1.19 us
  transfers between devices with their start and end apart: 3, of which 3 were waited for; matrix products, arithmetic and copies ran while one was open for 0% of the time, Pallas kernels for 8%

profile of v2, /device:TPU:0, one launch (start us, length us, event | category | flops | bytes accessed | tf_op | source)
XLA Modules:
  0.0 33.7 jit_solution(5948102229288140376)
XLA Ops:
  0.0 0.0 copy-start
  0.0 0.7 %copy-done = f32[2,2,512]{2,1,0:T(2,128)S(1)} copy-done((f32[2,2,512]{2,1,0:T(2,128)S(1)}, f32[2,2,512]{2,1,0:T(2,128)}, u32[]{:S(2)}) %copy-start) | copy-done | bytes 8216
  0.7 0.0 copy-start.1
  0.7 0.7 %copy-done.1 = s32[2,2,512]{2,1,0:T(2,128)S(1)} copy-done((s32[2,2,512]{2,1,0:T(2,128)S(1)}, s32[2,2,512]{2,1,0:T(2,128)}, u32[]{:S(2)}) %copy-start.1) | copy-done | bytes 8216
  1.4 0.0 copy-start.2
  1.4 0.7 %copy-done.2 = f32[2,512]{1,0:T(2,128)S(1)} copy-done((f32[2,512]{1,0:T(2,128)S(1)}, f32[2,512]{1,0:T(2,128)}, u32[]{:S(2)}) %copy-start.2) | copy-done | bytes 4120
  2.1 0.0 copy-start.3
  2.1 0.7 %copy-done.3 = s32[2,512]{1,0:T(2,128)S(1)} copy-done((s32[2,512]{1,0:T(2,128)S(1)}, s32[2,512]{1,0:T(2,128)}, u32[]{:S(2)}) %copy-start.3) | copy-done | bytes 4120
  2.8 0.4 %shard_map.73 = f32[16,16,128]{2,1,0:T(8,128)S(1)} custom-call(f32[2,2,512]{2,1,0:T(2,128)S(1)} %copy-done, f32[2,512]{1,0:T(2,128)S(1)} %copy-done.2, s32[2,2,512]{2,1,0:T(2,128)S(1)} %copy-done.1, s32[2,512]{1,0:T(2,128)S(1)} %copy-done.3), custom_call_target="tpu_custom_call" | custom-call | tf_op jit(solution)/shard_map/pallas_call | solution.py:242
  3.2 14.9 %all_to_all.5 = f32[16,16,128]{2,1,0:T(8,128)S(1)} all-to-all(f32[16,16,128]{2,1,0:T(8,128)S(1)} %shard_map.73), channel_id=1, replica_groups={{0,2,4,6,8,10,12,14,16,18,20,22,24,26,28,30},{1,3,5,7,9,11,13,15,17,19,..., dimensions={0} | all-to-all | bytes 262144 | tf_op jit(solution)/shard_map/all_to_all | solution.py:251
  18.2 0.0 copy-start.4
  18.2 0.0 copy-start.5
  18.2 3.9 %collective-permute-start = (f32[256,128]{1,0:T(8,128)S(1)}, f32[256,128]{1,0:T(8,128)S(1)}, u32[]{:S(2)}, u32[]{:S(2)}) collective-permute-start(f32[256,128]{1,0:T(8,128)S(1)} %bitcast.4), channel_id=1, source_target_pairs={{0,1},{1,0},{2,3},{3,2},{4,5},{5,4},{6,7},{7,6},{8,9},{9,8},{10,11... | collective-permute-start | bytes 393224 | tf_op jit(solution)/shard_map/ppermute | solution.py:253
  22.0 0.0 copy-done.4
  22.0 0.0 copy-done.5
  22.1 0.0 copy-done.6
  22.1 2.8 %shard_map.74 = (f32[64,128]{1,0:T(8,128)S(1)}, f32[64,128]{1,0:T(8,128)S(1)}) custom-call(s32[1,2]{1,0:T(1,128)S(1)} %copy-done.4, s32[1,64]{1,0:T(1,128)S(1)} %bitcast.6, f32[1,64]{1,0:T(1,128)S(1)} %copy-done.6, f32[256,128]{1,0:T(8,128)S(1)} %bitcast.5), custom_call_target="tpu_custom_call" | custom-call | flops 268435456 | bytes 262144 | tf_op jit(solution)/shard_map/pallas_call | solution.py:265
  24.9 0.1 collective-permute-done.data_ref
  25.0 2.9 %shard_map.75 = (f32[64,128]{1,0:T(8,128)S(1)}, f32[64,128]{1,0:T(8,128)S(1)}) custom-call(s32[1,2]{1,0:T(1,128)S(1)} %copy-done.4, s32[1,64]{1,0:T(1,128)S(1)} %bitcast.7, f32[1,64]{1,0:T(1,128)S(1)} %copy-done.6, f32[256,128]{1,0:T(8,128)S(1)} %collective-permute-done.data_ref, f32[64,128]{1,0:T(8,128)S(1)} %get-tuple-element.9.even_ref, ...), custom_call_target="tpu_custom_call" | custom-call | flops 268435456 | bytes 262144 | tf_op jit(solution)/shard_map/pallas_call | solution.py:274
  27.9 0.1 collective-permute-start.1
  28.0 1.2 %collective-permute-done.1 = f32[64,128]{1,0:T(8,128)S(1)} collective-permute-done((f32[64,128]{1,0:T(8,128)S(1)}, f32[64,128]{1,0:T(8,128)S(1)}, u32[]{:S(2)}, u32[]{:S(2)}) %collective-permute-start.1) | collective-permute-done | bytes 32800 | tf_op jit(solution)/shard_map/ppermute | solution.py:283
  29.2 1.6 %collective-permute-start.2 = (f32[32,128]{1,0:T(8,128)S(1)}, f32[32,128]{1,0:T(8,128)S(1)}, u32[]{:S(2)}, u32[]{:S(2)}) collective-permute-start(f32[32,128]{1,0:T(8,128)S(1)} %slice.9), channel_id=1, source_target_pairs={{0,64},{32,96},{64,0},{96,32},{1,65},{33,97},{65,1},{97,33},{2,66}... | collective-permute-start | bytes 49160 | tf_op jit(solution)/shard_map/ppermute | solution.py:284
  30.9 2.2 %collective-permute-done.2 = f32[32,128]{1,0:T(8,128)S(1)} collective-permute-done((f32[32,128]{1,0:T(8,128)S(1)}, f32[32,128]{1,0:T(8,128)S(1)}, u32[]{:S(2)}, u32[]{:S(2)}) %collective-permute-start.2) | collective-permute-done | bytes 16416 | tf_op jit(solution)/shard_map/ppermute | solution.py:284
  33.0 0.6 %fusion = f32[1,32,128]{2,1,0:T(8,128)} fusion(f32[32,128]{1,0:T(8,128)S(1)} %collective-permute-done.2, f32[64,128]{1,0:T(8,128)S(1)} %add.6), kind=kLoop, calls=%fused_computation.1 | loop fusion | flops 4096 | bytes 49152 | tf_op jit(solution)/shard_map/broadcast_in_dim | solution.py:284
  (3 shorter events, 0.0 us)
Async XLA Ops:
  0.0 0.7 %copy-start = (f32[2,2,512]{2,1,0:T(2,128)S(1)}, f32[2,2,512]{2,1,0:T(2,128)}, u32[]{:S(2)}) copy-start(f32[2,2,512]{2,1,0:T(2,128)} %vis_ref.1) | copy-start | bytes 24580
  0.7 0.7 %copy-start.1 = (s32[2,2,512]{2,1,0:T(2,128)S(1)}, s32[2,2,512]{2,1,0:T(2,128)}, u32[]{:S(2)}) copy-start(s32[2,2,512]{2,1,0:T(2,128)} %uv_ref.1) | copy-start | bytes 24580
  1.4 0.7 %copy-start.2 = (f32[2,512]{1,0:T(2,128)S(1)}, f32[2,512]{1,0:T(2,128)}, u32[]{:S(2)}) copy-start(f32[2,512]{1,0:T(2,128)} %weight_ref.1) | copy-start | bytes 12292
  2.1 0.7 %copy-start.3 = (s32[2,512]{1,0:T(2,128)S(1)}, s32[2,512]{1,0:T(2,128)}, u32[]{:S(2)}) copy-start(s32[2,512]{1,0:T(2,128)} %flag_ref.1) | copy-start | bytes 12292
  18.2 3.9 %copy-start.4 = (s32[1,2]{1,0:T(1,128)S(1)}, s32[1,2]{1,0:T(1,128)}, u32[]{:S(2)}) copy-start(s32[1,2]{1,0:T(1,128)} %facet_ref.3) | copy-start | bytes 28
  18.2 3.9 %copy-start.5 = (s32[64]{0:T(128)S(1)}, s32[64]{0:T(128)}, u32[]{:S(2)}) copy-start(s32[64]{0:T(128)} %param.11) | copy-start | bytes 772
  18.2 3.9 %copy-start.6 = (f32[1,64]{1,0:T(1,128)S(1)}, f32[1,64]{1,0:T(1,128)}, u32[]{:S(2)}) copy-start(f32[1,64]{1,0:T(1,128)} %beam_ref.3) | copy-start | bytes 772
  18.2 6.8 %collective-permute-start = (f32[256,128]{1,0:T(8,128)S(1)}, f32[256,128]{1,0:T(8,128)S(1)}, u32[]{:S(2)}, u32[]{:S(2)}) collective-permute-start(f32[256,128]{1,0:T(8,128)S(1)} %bitcast.4), channel_id=1, source_target_pairs={{0,1},{1,0},{2,3},{3,2},{4,5},{5,4},{6,7},{7,6},{8,9},{9,8},{10,11... | collective-permute-start | bytes 393224 | tf_op jit(solution)/shard_map/ppermute | solution.py:253
  27.9 1.3 %collective-permute-start.1 = (f32[64,128]{1,0:T(8,128)S(1)}, f32[64,128]{1,0:T(8,128)S(1)}, u32[]{:S(2)}, u32[]{:S(2)}) collective-permute-start(f32[64,128]{1,0:T(8,128)S(1)} %get-tuple-element.12), channel_id=1, source_target_pairs={{0,32},{32,0},{64,96},{96,64},{1,33},{33,1},{65,97},{97,65},{2,34}... | collective-permute-start | bytes 98312 | tf_op jit(solution)/shard_map/ppermute | solution.py:283
  29.2 3.8 %collective-permute-start.2 = (f32[32,128]{1,0:T(8,128)S(1)}, f32[32,128]{1,0:T(8,128)S(1)}, u32[]{:S(2)}, u32[]{:S(2)}) collective-permute-start(f32[32,128]{1,0:T(8,128)S(1)} %slice.9), channel_id=1, source_target_pairs={{0,64},{32,96},{64,0},{96,32},{1,65},{33,97},{65,1},{97,33},{2,66}... | collective-permute-start | bytes 49160 | tf_op jit(solution)/shard_map/ppermute | solution.py:284

commit v3 on v2

--- a/solution.py
+++ b/solution.py
@@ -29,7 +29,24 @@
     return jnp.concatenate(parts, axis=1)
 
 
-def pack_kernel(copies, vis_ref, weight_ref, uv_ref, flag_ref, out_ref, data_ref):
+def pack_kernel(
+    vis_in, weight_in, uv_in, flag_in, plan_in, beam_in, facet_in,
+    out_ref, gain_ref, centre_ref,
+    vis_ref, weight_ref, uv_ref, flag_ref, plan_ref, beam_ref, facet_ref, data_ref, arrived,
+):
+    copies = [
+        pltpu.make_async_copy(source, target, arrived.at[index])
+        for index, (source, target) in enumerate(
+            (
+                (flag_in, flag_ref), (vis_in, vis_ref), (weight_in, weight_ref), (uv_in, uv_ref),
+                (plan_in, plan_ref), (beam_in, beam_ref), (facet_in, facet_ref),
+            )
+        )
+    ]
+    for copy in copies:
+        copy.start()
+    for copy in copies:
+        copy.wait()
     rows = weight_ref.shape[1]
     flags = flag_ref[...].astype(jnp.float32)
     weights = weight_ref[...]
@@ -54,9 +71,22 @@
         packed.append(moved[0:8] + moved[8:16] + moved[16:24])
     parity = lax.broadcasted_iota(jnp.int32, packed[0].shape, 0) & 1
     result = jnp.where(parity == 0, packed[0], packed[1])
-    for copy in range(copies):
-        out_ref[copy, 0:8, :] = result[:, :LANES]
-        out_ref[copy, 8:16, :] = result[:, LANES:]
+    plane = out_ref.shape[0]
+    for peer in range(plane):
+        out_ref[peer, 0:8, :] = result[:, :LANES]
+        out_ref[peer, 8:16, :] = result[:, LANES:]
+    side = lax.axis_index("facet") & 1
+    shape = (plane, plan_ref.shape[1])
+    for which in range(2):
+        for member in range(2):
+            block = 4 * lax.broadcasted_iota(jnp.int32, shape, 0) + 2 * (side ^ which) + member
+            matches = plan_ref[...] == block
+            gain = jnp.sum(jnp.where(matches, beam_ref[...], 0.0), axis=1, keepdims=True)
+            first = (2 * which + member) * plane
+            gain_ref[first : first + plane, :] = jnp.broadcast_to(gain, (plane, LANES))
+    for axis in range(2):
+        centre = 2 * (facet_ref[0:1, axis : axis + 1] * P_SIZE - IMG // 2) + (P_SIZE - 1)
+        centre_ref[8 * axis : 8 * axis + 8, :] = jnp.broadcast_to(centre, (8, LANES))
 
 
 def doubled(sine, cosine):
@@ -97,12 +127,13 @@
     )
 
 
-def prepare(centre, data_ref, gain_ref, step, half, buffers):
+def prepare(which, centre_ref, data_ref, gain_ref, step, half, buffers):
     fine_v, fine_u, outer, coarse = buffers
-    column, row = centre
+    column, row = centre_ref[0:8, :], centre_ref[8:16, :]
     tile = step >> 1
     member = step & 1
-    gain = gain_ref[pl.ds(pl.multiple_of(member * (gain_ref.shape[0] // 2) + tile * 8, 8), 8), :]
+    owners = gain_ref.shape[0] // 4
+    gain = gain_ref[pl.ds(pl.multiple_of((2 * which + member) * owners + tile * 8, 8), 8), :]
     first = tile * 128 + 8 * half + member
     real, imag, u, v = (
         data_ref[pl.ds(first + 2 * kind, 8, stride=16), :] for kind in range(4)
@@ -163,48 +194,34 @@
     return values
 
 
-def sum_blocks(block_of, facet_ref, plan_ref, beam_ref, data_ref, scratch, sums):
-    gain_ref, buffers = scratch[0], (scratch[1:5], scratch[5:9])
-    owners = data_ref.shape[0] // 16
-    centre = tuple(2 * (facet_ref[0, k] * P_SIZE - IMG // 2) + (P_SIZE - 1) for k in range(2))
-    for member in range(2):
-        owner = lax.broadcasted_iota(jnp.int32, (owners, plan_ref.shape[1]), 0)
-        matches = plan_ref[...] == block_of(owner, member)
-        gain = jnp.sum(jnp.where(matches, beam_ref[...], 0.0), axis=1, keepdims=True)
-        gain_ref[member * owners : (member + 1) * owners, :] = jnp.broadcast_to(
-            gain, (owners, LANES)
-        )
-    steps = owners // 4
-    prepare(centre, data_ref, gain_ref, 0, 0, buffers[0])
+def sum_blocks(which, centre_ref, gain_ref, data_ref, scratch, sums):
+    buffers = (scratch[0:4], scratch[4:8])
+    source = (which, centre_ref, data_ref, gain_ref)
+    steps = data_ref.shape[0] // 64
+    prepare(*source, 0, 0, buffers[0])
 
     def advance(step, sums):
-        prepare(centre, data_ref, gain_ref, step, 1, buffers[1])
+        prepare(*source, step, 1, buffers[1])
         sums = accumulate(buffers[0], sums)
-        prepare(centre, data_ref, gain_ref, (step + 1) & (steps - 1), 0, buffers[0])
+        prepare(*source, (step + 1) & (steps - 1), 0, buffers[0])
         return accumulate(buffers[1], sums)
 
     return lax.fori_loop(0, steps, advance, sums)
 
 
-def first_kernel(facet_ref, plan_ref, beam_ref, data_ref, even_ref, odd_ref, *scratch):
-    side = lax.axis_index("facet") & 1
+def first_kernel(centre_ref, gain_ref, data_ref, even_ref, odd_ref, *scratch):
     zero = jnp.zeros((HALF, P_SIZE), jnp.float32)
-    even, odd = sum_blocks(
-        lambda owner, member: 4 * owner + 2 * side + member,
-        facet_ref, plan_ref, beam_ref, data_ref, scratch, (zero, zero),
-    )
+    even, odd = sum_blocks(0, centre_ref, gain_ref, data_ref, scratch, (zero, zero))
     even_ref[...] = even
     odd_ref[...] = odd
 
 
 def last_kernel(
-    scale, facet_ref, plan_ref, beam_ref, data_ref, even_ref, odd_ref, keep_ref, send_ref,
+    scale, centre_ref, gain_ref, data_ref, even_ref, odd_ref, keep_ref, send_ref,
     order_ref, *scratch,
 ):
-    side = 1 - (lax.axis_index("facet") & 1)
     even, odd = sum_blocks(
-        lambda owner, member: 4 * owner + 2 * side + member,
-        facet_ref, plan_ref, beam_ref, data_ref, scratch, (even_ref[...], odd_ref[...]),
+        1, centre_ref, gain_ref, data_ref, scratch, (even_ref[...], odd_ref[...])
     )
     even, odd = even * scale, odd * scale
     core = lax.axis_index("freq") & 1
@@ -235,18 +252,26 @@
 
 SMALL = pltpu.CompilerParams(vmem_limit_bytes=8 << 20)
 VMEM = pl.BlockSpec(memory_space=pltpu.VMEM)
-SMEM = pl.BlockSpec(memory_space=pltpu.SMEM)
 
 
 def body(total, plane, visibilities, weights, uv_cells, flags, plan, beam, facets):
-    packed = pl.pallas_call(
-        functools.partial(pack_kernel, plane),
-        out_shape=jax.ShapeDtypeStruct((plane, 16, LANES), jnp.float32),
-        in_specs=[VMEM] * 4,
-        out_specs=VMEM,
-        scratch_shapes=[pltpu.VMEM((8, weights.shape[1]), jnp.float32)],
+    arguments = (visibilities, weights, uv_cells, flags, plan[None], beam, facets)
+    packed, gains, centre = pl.pallas_call(
+        pack_kernel,
+        out_shape=(
+            jax.ShapeDtypeStruct((plane, 16, LANES), jnp.float32),
+            jax.ShapeDtypeStruct((4 * plane, LANES), jnp.float32),
+            jax.ShapeDtypeStruct((16, LANES), jnp.int32),
+        ),
+        in_specs=[pl.BlockSpec(memory_space=pltpu.HBM)] * 7,
+        out_specs=(VMEM, VMEM, VMEM),
+        scratch_shapes=[pltpu.VMEM(each.shape, each.dtype) for each in arguments]
+        + [
+            pltpu.VMEM((8, weights.shape[1]), jnp.float32),
+            pltpu.SemaphoreType.DMA((len(arguments),)),
+        ],
         compiler_params=SMALL,
-    )(visibilities, weights, uv_cells, flags)
+    )(*(pltpu.with_memory_space_constraint(each, pltpu.HBM) for each in arguments))
     groups = [list(range(side, 2 * plane, 2)) for side in range(2)]
     near = lax.all_to_all(packed, "facet", 0, 0, axis_index_groups=groups)
     near = near.reshape(plane * 16, LANES)
@@ -258,28 +283,28 @@
         pltpu.VMEM((16, 8, LANES), jnp.float32),
         pltpu.VMEM((8, 8, LANES), jnp.float32),
     ]
-    scratch = [pltpu.VMEM((2 * plane, LANES), jnp.float32)] + buffers * 2
+    scratch = buffers * 2
     cost = pl.CostEstimate(
         flops=2 * 2 * HALF * P_SIZE * 2 * plane * KEEP, bytes_accessed=1 << 18, transcendentals=0
     )
     even, odd = pl.pallas_call(
         first_kernel,
         out_shape=(image, image),
-        in_specs=[SMEM, VMEM, VMEM, VMEM],
+        in_specs=[VMEM] * 3,
         out_specs=(VMEM, VMEM),
         scratch_shapes=scratch,
         compiler_params=SMALL,
         cost_estimate=cost,
-    )(facets, plan[None], beam, near)
+    )(centre, gains, near)
     keep, send = pl.pallas_call(
         functools.partial(last_kernel, 2.0 / math.sqrt(total)),
         out_shape=(image, image),
-        in_specs=[SMEM, VMEM, VMEM, VMEM, VMEM, VMEM],
+        in_specs=[VMEM] * 5,
         out_specs=(VMEM, VMEM),
         scratch_shapes=[pltpu.VMEM((P_SIZE, P_SIZE), jnp.float32)] + scratch,
         compiler_params=SMALL,
         cost_estimate=cost,
-    )(facets, plan[None], beam, far, even, odd)
+    )(centre, gains, far, even, odd)
     half = keep + lax.ppermute(send, "freq", [(i, i ^ 1) for i in range(4)])
     return (half[:32] + lax.ppermute(half[32:], "freq", [(i, i ^ 2) for i in range(4)]))[None]
 

time: 33.9 us -> 31.3 us (0.923)
  local copies, waits for them, and re-layouts: 2.78 us -> 0.01 us
  waiting for transfers between devices: 3.5 us -> 4.1 us
  Pallas kernels: 6.17 us -> 5.79 us
    unnamed x14 -> x0, local copies, waits for them, and re-layouts: 2.78 us -> none
    ppermute x1, waiting for transfers between devices: 0.14 us -> 0.74 us  [body(): far = lax.ppermute(near, 'facet', [(i, i ^ 1) for i in range(2 * plane)])]
    pallas_call x1, Pallas kernels: 2.93 us -> 2.34 us  [body(): pl.pallas_call(functools.partial(last_kernel, 2.0 / math.sqrt(total)), ou...]
  transfers between devices with their start and end apart: 3 -> 3, of which waited for: 3 -> 3; matrix products, arithmetic and copies ran while one was open for 0% -> 0% of each run, Pallas kernels for 8% -> 7%
where the time goes in v3:
time: 31.3 us; the launch traced here: 31.1 us
  blocking collectives  14.9 us (48%)
  Pallas kernels  5.79 us (18%)
  starting transfers between devices  5.61 us (18%)
  waiting for transfers between devices  4.1 us (13%)
  other arithmetic  0.61 us (2%)
    all_to_all x1, blocking collectives, body(): near = lax.all_to_all(packed, 'facet', 0, 0, axis_index_groups=groups)  14.9 us
    ppermute x1, starting transfers between devices, body(): far = lax.ppermute(near, 'facet', [(i, i ^ 1) for i in range(2 * plane)])  3.88 us
    pallas_call x1, Pallas kernels, body(): pl.pallas_call(functools.partial(last_kernel, 2.0 / math.sqrt(total)), ou...  2.34 us
    pallas_call x1, Pallas kernels, body(): pl.pallas_call(first_kernel, out_shape=(image, image), in_specs=[VMEM] *...  2.2 us
    ppermute x1, waiting for transfers between devices, body(): lax.ppermute(half[32:], 'freq', [(i, i ^ 2) for i in range(4)])  2.17 us
    ppermute x1, starting transfers between devices, body(): lax.ppermute(half[32:], 'freq', [(i, i ^ 2) for i in range(4)])  1.65 us
    pallas_call x1, Pallas kernels, body(): pl.pallas_call(pack_kernel, out_shape=(jax.ShapeDtypeStruct((plane, 16, L...  1.26 us
    ppermute x1, waiting for transfers between devices, body(): half = keep + lax.ppermute(send, 'freq', [(i, i ^ 1) for i in range(4)])  1.19 us
  transfers between devices with their start and end apart: 3, of which 3 were waited for; matrix products, arithmetic and copies ran while one was open for 0% of the time, Pallas kernels for 7%

profile of v3, /device:TPU:0, one launch (start us, length us, event | category | flops | bytes accessed | tf_op | source)
XLA Modules:
  0.0 31.1 jit_solution(10540559627652115348)
XLA Ops:
  0.0 1.3 %shard_map.73 = (f32[16,16,128]{2,1,0:T(8,128)S(1)}, f32[64,128]{1,0:T(8,128)S(1)}, s32[16,128]{1,0:T(8,128)S(1)}) custom-call(f32[2,2,512]{2,1,0:T(2,128)} %vis_in.1, f32[2,512]{1,0:T(2,128)} %weight_in.1, s32[2,2,512]{2,1,0:T(2,128)} %uv_in.1, s32[2,512]{1,0:T(2,128)} %flag_in.1, s32[1,64]{1,0:T(1,128)} %bitcast.6, f32[1,64]{1,0:T(1,128)} %beam_in.1, ...), custom_call_target="tpu_custom_call" | custom-call | tf_op jit(solution)/shard_map/pallas_call | solution.py:259
  1.3 14.9 %all_to_all.5 = f32[16,16,128]{2,1,0:T(8,128)S(1)} all-to-all(f32[16,16,128]{2,1,0:T(8,128)S(1)} %get-tuple-element.14), channel_id=1, replica_groups={{0,2,4,6,8,10,12,14,16,18,20,22,24,26,28,30},{1,3,5,7,9,11,13,15,17,19,..., dimensions={0} | all-to-all | bytes 262144 | tf_op jit(solution)/shard_map/all_to_all | solution.py:276
  16.2 3.9 %collective-permute-start = (f32[256,128]{1,0:T(8,128)S(1)}, f32[256,128]{1,0:T(8,128)S(1)}, u32[]{:S(2)}, u32[]{:S(2)}) collective-permute-start(f32[256,128]{1,0:T(8,128)S(1)} %bitcast.4), channel_id=1, source_target_pairs={{0,1},{1,0},{2,3},{3,2},{4,5},{5,4},{6,7},{7,6},{8,9},{9,8},{10,11... | collective-permute-start | bytes 393224 | tf_op jit(solution)/shard_map/ppermute | solution.py:278
  20.1 2.2 %shard_map.74 = (f32[64,128]{1,0:T(8,128)S(1)}, f32[64,128]{1,0:T(8,128)S(1)}) custom-call(s32[16,128]{1,0:T(8,128)S(1)} %get-tuple-element.12.centre_ref, f32[64,128]{1,0:T(8,128)S(1)} %get-tuple-element.13.gain_ref, f32[256,128]{1,0:T(8,128)S(1)} %bitcast.5), custom_call_target="tpu_custom_call" | custom-call | flops 268435456 | bytes 262144 | tf_op jit(solution)/shard_map/pallas_call | solution.py:290
  22.3 0.7 %collective-permute-done.data_ref = f32[256,128]{1,0:T(8,128)S(1)} collective-permute-done((f32[256,128]{1,0:T(8,128)S(1)}, f32[256,128]{1,0:T(8,128)S(1)}, u32[]{:S(2)}, u32[]{:S(2)}) %collective-permute-start) | collective-permute-done | bytes 131104 | tf_op jit(solution)/shard_map/ppermute | solution.py:278
  23.0 2.3 %shard_map.75 = (f32[64,128]{1,0:T(8,128)S(1)}, f32[64,128]{1,0:T(8,128)S(1)}) custom-call(s32[16,128]{1,0:T(8,128)S(1)} %get-tuple-element.12.centre_ref, f32[64,128]{1,0:T(8,128)S(1)} %get-tuple-element.13.gain_ref, f32[256,128]{1,0:T(8,128)S(1)} %collective-permute-done.data_ref, f32[64,128]{1,0:T(8,128)S(1)} %get-tuple-element.15.even_ref, ...), custom_call_target="tpu_custom_call" | custom-call | flops 268435456 | bytes 262144 | tf_op jit(solution)/shard_map/pallas_call | solution.py:299
  25.4 0.1 collective-permute-start.1
  25.5 1.2 %collective-permute-done.1 = f32[64,128]{1,0:T(8,128)S(1)} collective-permute-done((f32[64,128]{1,0:T(8,128)S(1)}, f32[64,128]{1,0:T(8,128)S(1)}, u32[]{:S(2)}, u32[]{:S(2)}) %collective-permute-start.1) | collective-permute-done | bytes 32800 | tf_op jit(solution)/shard_map/ppermute | solution.py:308
  26.7 1.6 %collective-permute-start.2 = (f32[32,128]{1,0:T(8,128)S(1)}, f32[32,128]{1,0:T(8,128)S(1)}, u32[]{:S(2)}, u32[]{:S(2)}) collective-permute-start(f32[32,128]{1,0:T(8,128)S(1)} %slice.9), channel_id=1, source_target_pairs={{0,64},{32,96},{64,0},{96,32},{1,65},{33,97},{65,1},{97,33},{2,66}... | collective-permute-start | bytes 49160 | tf_op jit(solution)/shard_map/ppermute | solution.py:309
  28.3 2.2 %collective-permute-done.2 = f32[32,128]{1,0:T(8,128)S(1)} collective-permute-done((f32[32,128]{1,0:T(8,128)S(1)}, f32[32,128]{1,0:T(8,128)S(1)}, u32[]{:S(2)}, u32[]{:S(2)}) %collective-permute-start.2) | collective-permute-done | bytes 16416 | tf_op jit(solution)/shard_map/ppermute | solution.py:309
  30.5 0.6 %fusion = f32[1,32,128]{2,1,0:T(8,128)} fusion(f32[32,128]{1,0:T(8,128)S(1)} %collective-permute-done.2, f32[64,128]{1,0:T(8,128)S(1)} %add.6), kind=kLoop, calls=%fused_computation.1 | loop fusion | flops 4096 | bytes 49152 | tf_op jit(solution)/shard_map/broadcast_in_dim | solution.py:309
  (2 shorter events, 0.0 us)
Async XLA Ops:
  16.2 6.8 %collective-permute-start = (f32[256,128]{1,0:T(8,128)S(1)}, f32[256,128]{1,0:T(8,128)S(1)}, u32[]{:S(2)}, u32[]{:S(2)}) collective-permute-start(f32[256,128]{1,0:T(8,128)S(1)} %bitcast.4), channel_id=1, source_target_pairs={{0,1},{1,0},{2,3},{3,2},{4,5},{5,4},{6,7},{7,6},{8,9},{9,8},{10,11... | collective-permute-start | bytes 393224 | tf_op jit(solution)/shard_map/ppermute | solution.py:278
  25.4 1.3 %collective-permute-start.1 = (f32[64,128]{1,0:T(8,128)S(1)}, f32[64,128]{1,0:T(8,128)S(1)}, u32[]{:S(2)}, u32[]{:S(2)}) collective-permute-start(f32[64,128]{1,0:T(8,128)S(1)} %get-tuple-element.18), channel_id=1, source_target_pairs={{0,32},{32,0},{64,96},{96,64},{1,33},{33,1},{65,97},{97,65},{2,34}... | collective-permute-start | bytes 98312 | tf_op jit(solution)/shard_map/ppermute | solution.py:308
  26.7 3.8 %collective-permute-start.2 = (f32[32,128]{1,0:T(8,128)S(1)}, f32[32,128]{1,0:T(8,128)S(1)}, u32[]{:S(2)}, u32[]{:S(2)}) collective-permute-start(f32[32,128]{1,0:T(8,128)S(1)} %slice.9), channel_id=1, source_target_pairs={{0,64},{32,96},{64,0},{96,32},{1,65},{33,97},{65,1},{97,33},{2,66}... | collective-permute-start | bytes 49160 | tf_op jit(solution)/shard_map/ppermute | solution.py:309

commit v4 on v3

--- a/solution.py
+++ b/solution.py
@@ -31,7 +31,7 @@
 
 def pack_kernel(
     vis_in, weight_in, uv_in, flag_in, plan_in, beam_in, facet_in,
-    out_ref, gain_ref, centre_ref,
+    out_ref, mine_ref, other_ref,
     vis_ref, weight_ref, uv_ref, flag_ref, plan_ref, beam_ref, facet_ref, data_ref, arrived,
 ):
     copies = [
@@ -77,16 +77,18 @@
         out_ref[peer, 8:16, :] = result[:, LANES:]
     side = lax.axis_index("facet") & 1
     shape = (plane, plan_ref.shape[1])
-    for which in range(2):
+    for which, note_ref in ((0, mine_ref), (1, other_ref)):
+        for axis in range(2):
+            centre = 2 * (facet_ref[0:1, axis : axis + 1] * P_SIZE - IMG // 2) + (P_SIZE - 1)
+            note_ref[8 * axis : 8 * axis + 8, :] = jnp.broadcast_to(
+                centre.astype(jnp.float32), (8, LANES)
+            )
         for member in range(2):
             block = 4 * lax.broadcasted_iota(jnp.int32, shape, 0) + 2 * (side ^ which) + member
             matches = plan_ref[...] == block
             gain = jnp.sum(jnp.where(matches, beam_ref[...], 0.0), axis=1, keepdims=True)
-            first = (2 * which + member) * plane
-            gain_ref[first : first + plane, :] = jnp.broadcast_to(gain, (plane, LANES))
-    for axis in range(2):
-        centre = 2 * (facet_ref[0:1, axis : axis + 1] * P_SIZE - IMG // 2) + (P_SIZE - 1)
-        centre_ref[8 * axis : 8 * axis + 8, :] = jnp.broadcast_to(centre, (8, LANES))
+            first = 16 + member * plane
+            note_ref[first : first + plane, :] = jnp.broadcast_to(gain, (plane, LANES))
 
 
 def doubled(sine, cosine):
@@ -127,13 +129,14 @@
     )
 
 
-def prepare(which, centre_ref, data_ref, gain_ref, step, half, buffers):
+def prepare(note_ref, data_ref, step, half, buffers):
     fine_v, fine_u, outer, coarse = buffers
-    column, row = centre_ref[0:8, :], centre_ref[8:16, :]
+    column = note_ref[0:8, :].astype(jnp.int32)
+    row = note_ref[8:16, :].astype(jnp.int32)
     tile = step >> 1
     member = step & 1
-    owners = gain_ref.shape[0] // 4
-    gain = gain_ref[pl.ds(pl.multiple_of((2 * which + member) * owners + tile * 8, 8), 8), :]
+    place = 16 + member * (data_ref.shape[0] // 16) + tile * 8
+    gain = note_ref[pl.ds(pl.multiple_of(place, 8), 8), :]
     first = tile * 128 + 8 * half + member
     real, imag, u, v = (
         data_ref[pl.ds(first + 2 * kind, 8, stride=16), :] for kind in range(4)
@@ -194,38 +197,22 @@
     return values
 
 
-def sum_blocks(which, centre_ref, gain_ref, data_ref, scratch, sums):
+def image_kernel(scale, swap, note_ref, data_ref, image_ref, *scratch):
     buffers = (scratch[0:4], scratch[4:8])
-    source = (which, centre_ref, data_ref, gain_ref)
     steps = data_ref.shape[0] // 64
-    prepare(*source, 0, 0, buffers[0])
+    prepare(note_ref, data_ref, 0, 0, buffers[0])
 
     def advance(step, sums):
-        prepare(*source, step, 1, buffers[1])
+        prepare(note_ref, data_ref, step, 1, buffers[1])
         sums = accumulate(buffers[0], sums)
-        prepare(*source, (step + 1) & (steps - 1), 0, buffers[0])
+        prepare(note_ref, data_ref, (step + 1) & (steps - 1), 0, buffers[0])
         return accumulate(buffers[1], sums)
 
-    return lax.fori_loop(0, steps, advance, sums)
-
-
-def first_kernel(centre_ref, gain_ref, data_ref, even_ref, odd_ref, *scratch):
     zero = jnp.zeros((HALF, P_SIZE), jnp.float32)
-    even, odd = sum_blocks(0, centre_ref, gain_ref, data_ref, scratch, (zero, zero))
-    even_ref[...] = even
-    odd_ref[...] = odd
-
-
-def last_kernel(
-    scale, centre_ref, gain_ref, data_ref, even_ref, odd_ref, keep_ref, send_ref,
-    order_ref, *scratch,
-):
-    even, odd = sum_blocks(
-        1, centre_ref, gain_ref, data_ref, scratch, (even_ref[...], odd_ref[...])
-    )
+    even, odd = lax.fori_loop(0, steps, advance, (zero, zero))
     even, odd = even * scale, odd * scale
     core = lax.axis_index("freq") & 1
-    far = lax.axis_index("freq") >> 1
+    far = (lax.axis_index("freq") >> 1) ^ swap
     lane = lax.broadcasted_iota(jnp.int32, (8, P_SIZE), 1)
     near = jnp.where((lane & 8) == 8, lane ^ 8, lane ^ 7)
     sign = jnp.where((lane & 8) == 8, -1.0, 1.0)
@@ -245,9 +232,7 @@
             piece = index // 4
             slot = ((piece & 1) ^ core) * 2 + ((piece >> 1) ^ far)
             place = pl.multiple_of(slot * 32 + 8 * (index % 4), 8)
-            order_ref[pl.ds(place, 8), :] = values
-    keep_ref[...] = order_ref[0:HALF, :]
-    send_ref[...] = order_ref[HALF:, :]
+            image_ref[pl.ds(place, 8), :] = values
 
 
 SMALL = pltpu.CompilerParams(vmem_limit_bytes=8 << 20)
@@ -256,13 +241,10 @@
 
 def body(total, plane, visibilities, weights, uv_cells, flags, plan, beam, facets):
     arguments = (visibilities, weights, uv_cells, flags, plan[None], beam, facets)
-    packed, gains, centre = pl.pallas_call(
+    note = jax.ShapeDtypeStruct((16 + 2 * plane, LANES), jnp.float32)
+    packed, mine, other = pl.pallas_call(
         pack_kernel,
-        out_shape=(
-            jax.ShapeDtypeStruct((plane, 16, LANES), jnp.float32),
-            jax.ShapeDtypeStruct((4 * plane, LANES), jnp.float32),
-            jax.ShapeDtypeStruct((16, LANES), jnp.int32),
-        ),
+        out_shape=(jax.ShapeDtypeStruct((plane, 16, LANES), jnp.float32), note, note),
         in_specs=[pl.BlockSpec(memory_space=pltpu.HBM)] * 7,
         out_specs=(VMEM, VMEM, VMEM),
         scratch_shapes=[pltpu.VMEM(each.shape, each.dtype) for each in arguments]
@@ -272,11 +254,11 @@
         ],
         compiler_params=SMALL,
     )(*(pltpu.with_memory_space_constraint(each, pltpu.HBM) for each in arguments))
+    across = [(i, i ^ 65) for i in range(4 * 2 * plane)]
+    other = lax.ppermute(other, ("freq", "facet"), across)
     groups = [list(range(side, 2 * plane, 2)) for side in range(2)]
     near = lax.all_to_all(packed, "facet", 0, 0, axis_index_groups=groups)
     near = near.reshape(plane * 16, LANES)
-    far = lax.ppermute(near, "facet", [(i, i ^ 1) for i in range(2 * plane)])
-    image = jax.ShapeDtypeStruct((HALF, P_SIZE), jnp.float32)
     buffers = [
         pltpu.VMEM((2, 64, LANES), jnp.float32),
         pltpu.VMEM((2, 64, LANES), jnp.float32),
@@ -287,25 +269,21 @@
     cost = pl.CostEstimate(
         flops=2 * 2 * HALF * P_SIZE * 2 * plane * KEEP, bytes_accessed=1 << 18, transcendentals=0
     )
-    even, odd = pl.pallas_call(
-        first_kernel,
-        out_shape=(image, image),
-        in_specs=[VMEM] * 3,
-        out_specs=(VMEM, VMEM),
-        scratch_shapes=scratch,
-        compiler_params=SMALL,
-        cost_estimate=cost,
-    )(centre, gains, near)
-    keep, send = pl.pallas_call(
-        functools.partial(last_kernel, 2.0 / math.sqrt(total)),
-        out_shape=(image, image),
-        in_specs=[VMEM] * 5,
-        out_specs=(VMEM, VMEM),
-        scratch_shapes=[pltpu.VMEM((P_SIZE, P_SIZE), jnp.float32)] + scratch,
-        compiler_params=SMALL,
-        cost_estimate=cost,
-    )(centre, gains, far, even, odd)
-    half = keep + lax.ppermute(send, "freq", [(i, i ^ 1) for i in range(4)])
+
+    def image(swap, note):
+        return pl.pallas_call(
+            functools.partial(image_kernel, 2.0 / math.sqrt(total), swap),
+            out_shape=jax.ShapeDtypeStruct((P_SIZE, P_SIZE), jnp.float32),
+            in_specs=[VMEM] * 2,
+            out_specs=VMEM,
+            scratch_shapes=scratch,
+            compiler_params=SMALL,
+            cost_estimate=cost,
+        )(note, near)
+
+    joined = lax.ppermute(image(1, other), ("freq", "facet"), across)
+    joined = joined + image(0, mine)
+    half = joined[:HALF] + lax.ppermute(joined[HALF:], "freq", [(i, i ^ 1) for i in range(4)])
     return (half[:32] + lax.ppermute(half[32:], "freq", [(i, i ^ 2) for i in range(4)]))[None]
 
 

time: 31.3 us -> 31.8 us (1.016)
  blocking collectives: 14.9 us -> 0 us
  starting transfers between devices: 5.61 us -> 15.6 us
  waiting for transfers between devices: 4.1 us -> 8.79 us
  Pallas kernels: 5.79 us -> 6.55 us
    all_to_all x1 -> x0, blocking collectives: 14.9 us -> none  [body(): near = lax.all_to_all(packed, 'facet', 0, 0, axis_index_groups=groups)]
    all_to_all x0 -> x1, starting transfers between devices: none -> 7.16 us  [body(): near = lax.all_to_all(packed, 'facet', 0, 0, axis_index_groups=groups)]
    ppermute x2 -> x3, starting transfers between devices: 3.96 us -> 8.32 us  [the longest x1 4.12 us: body(): other = lax.ppermute(other, ('freq', 'facet'), across)]
    all_to_all x0 -> x1, waiting for transfers between devices: none -> 2.06 us  [body(): near = lax.all_to_all(packed, 'facet', 0, 0, axis_index_groups=groups)]
    ppermute x1, starting transfers between devices: 1.65 us -> 0.08 us  [body(): lax.ppermute(half[32:], 'freq', [(i, i ^ 2) for i in range(4)])]
    ppermute x1, waiting for transfers between devices: 2.17 us -> 3.73 us  [body(): lax.ppermute(half[32:], 'freq', [(i, i ^ 2) for i in range(4)])]
    ppermute x2 -> x3, waiting for transfers between devices: 1.93 us -> 3 us  [the longest x1 1.81 us: body(): other = lax.ppermute(other, ('freq', 'facet'), across)]
    pallas_call x1, Pallas kernels: 1.26 us -> 1.91 us  [body(): pl.pallas_call(pack_kernel, out_shape=(jax.ShapeDtypeStruct((plane, 16, L...]
  transfers between devices with their start and end apart: 3 -> 5, of which waited for: 3 -> 4; matrix products, arithmetic and copies ran while one was open for 0% -> 0% of each run, Pallas kernels for 7% -> 7%
where the time goes in v4:
time: 31.8 us; the launch traced here: 31.6 us
  starting transfers between devices  15.6 us (49%)
  waiting for transfers between devices  8.79 us (28%)
  Pallas kernels  6.55 us (21%)
  other arithmetic  0.62 us (2%)
    all_to_all x1, starting transfers between devices, body(): near = lax.all_to_all(packed, 'facet', 0, 0, axis_index_groups=groups)  7.16 us
    pallas_call x2, Pallas kernels, image(): pl.pallas_call(functools.partial(image_kernel, 2.0 / math.sqrt(total), sw...  4.64 us
    ppermute x1, starting transfers between devices, body(): other = lax.ppermute(other, ('freq', 'facet'), across)  4.12 us
    ppermute x1, starting transfers between devices, body(): joined = lax.ppermute(image(1, other), ('freq', 'facet'), across)  4.12 us
    ppermute x1, waiting for transfers between devices, body(): lax.ppermute(half[32:], 'freq', [(i, i ^ 2) for i in range(4)])  3.73 us
    all_to_all x1, waiting for transfers between devices, body(): near = lax.all_to_all(packed, 'facet', 0, 0, axis_index_groups=groups)  2.06 us
    pallas_call x1, Pallas kernels, body(): pl.pallas_call(pack_kernel, out_shape=(jax.ShapeDtypeStruct((plane, 16, L...  1.91 us
    ppermute x1, waiting for transfers between devices, body(): other = lax.ppermute(other, ('freq', 'facet'), across)  1.81 us
  transfers between devices with their start and end apart: 5, of which 4 were waited for; matrix products, arithmetic and copies ran while one was open for 0% of the time, Pallas kernels for 7%

profile of v4, /device:TPU:0, one launch (start us, length us, event | category | flops | bytes accessed | tf_op | source)
XLA Modules:
  0.0 31.6 jit_solution(5641194181335511638)
XLA Ops:
  0.0 1.9 %shard_map.73 = (f32[16,16,128]{2,1,0:T(8,128)}, f32[48,128]{1,0:T(8,128)S(1)}, f32[48,128]{1,0:T(8,128)S(1)}) custom-call(f32[2,2,512]{2,1,0:T(2,128)} %vis_in.1, f32[2,512]{1,0:T(2,128)} %weight_in.1, s32[2,2,512]{2,1,0:T(2,128)} %uv_in.1, s32[2,512]{1,0:T(2,128)} %flag_in.1, s32[1,64]{1,0:T(1,128)} %bitcast.6, f32[1,64]{1,0:T(1,128)} %beam_in.1, ...), custom_call_target="tpu_custom_call" | custom-call | tf_op jit(solution)/shard_map/pallas_call | solution.py:245
  1.9 7.2 %all-to-all-start = ((f32[16,16,128]{2,1,0:T(8,128)}), f32[16,16,128]{2,1,0:T(8,128)S(1)}, u32[]{:S(2)}, u32[]{:S(2)}) async-start(f32[16,16,128]{2,1,0:T(8,128)} %get-tuple-element.9), calls=%async_computation | async-start | bytes 262144 | tf_op jit(solution)/shard_map/all_to_all | solution.py:260
  9.1 4.1 %collective-permute-start = (f32[48,128]{1,0:T(8,128)S(1)}, f32[48,128]{1,0:T(8,128)S(1)}, u32[]{:S(2)}, u32[]{:S(2)}) collective-permute-start(f32[48,128]{1,0:T(8,128)S(1)} %get-tuple-element.8), channel_id=1, source_target_pairs={{0,65},{1,64},{2,67},{3,66},{4,69},{5,68},{6,71},{7,70},{8,73},{9,... | collective-permute-start | bytes 73736 | tf_op jit(solution)/shard_map/ppermute | solution.py:258
  13.2 1.8 %collective-permute-done.note_ref = f32[48,128]{1,0:T(8,128)S(1)} collective-permute-done((f32[48,128]{1,0:T(8,128)S(1)}, f32[48,128]{1,0:T(8,128)S(1)}, u32[]{:S(2)}, u32[]{:S(2)}) %collective-permute-start) | collective-permute-done | bytes 24608 | tf_op jit(solution)/shard_map/ppermute | solution.py:258
  15.0 2.1 %all-to-all-done = f32[16,16,128]{2,1,0:T(8,128)S(1)} async-done(((f32[16,16,128]{2,1,0:T(8,128)}), f32[16,16,128]{2,1,0:T(8,128)S(1)}, u32[]{:S(2)}, u32[]{:S(2)}) %all-to-all-start) | async-done | bytes 131104 | tf_op jit(solution)/shard_map/all_to_all | solution.py:260
  17.1 2.3 %shard_map.74 = f32[128,128]{1,0:T(8,128)S(1)} custom-call(f32[48,128]{1,0:T(8,128)S(1)} %collective-permute-done.note_ref, f32[256,128]{1,0:T(8,128)S(1)} %bitcast.4), custom_call_target="tpu_custom_call" | custom-call | flops 268435456 | bytes 262144 | tf_op jit(solution)/shard_map/pallas_call | solution.py:274
  19.4 4.1 %collective-permute-start.1 = (f32[128,128]{1,0:T(8,128)S(1)}, f32[128,128]{1,0:T(8,128)S(1)}, u32[]{:S(2)}, u32[]{:S(2)}) collective-permute-start(f32[128,128]{1,0:T(8,128)S(1)} %shard_map.74), channel_id=1, source_target_pairs={{0,65},{1,64},{2,67},{3,66},{4,69},{5,68},{6,71},{7,70},{8,73},{9,... | collective-permute-start | bytes 196616 | tf_op jit(solution)/shard_map/ppermute | solution.py:284
  23.5 2.3 %shard_map.75 = f32[128,128]{1,0:T(8,128)S(1)} custom-call(f32[48,128]{1,0:T(8,128)S(1)} %get-tuple-element.10.note_ref, f32[256,128]{1,0:T(8,128)S(1)} %bitcast.5), custom_call_target="tpu_custom_call" | custom-call | flops 268435456 | bytes 262144 | tf_op jit(solution)/shard_map/pallas_call | solution.py:274
  25.8 0.0 collective-permute-done.1
  25.9 0.1 collective-permute-start.2
  26.0 1.2 %collective-permute-done.2 = f32[64,128]{1,0:T(8,128)S(1)} collective-permute-done((f32[64,128]{1,0:T(8,128)S(1)}, f32[64,128]{1,0:T(8,128)S(1)}, u32[]{:S(2)}, u32[]{:S(2)}) %collective-permute-start.2) | collective-permute-done | bytes 32800 | tf_op jit(solution)/shard_map/ppermute | solution.py:286
  27.2 0.1 collective-permute-start.3
  27.3 3.7 %collective-permute-done.3 = f32[32,128]{1,0:T(8,128)S(1)} collective-permute-done((f32[32,128]{1,0:T(8,128)S(1)}, f32[32,128]{1,0:T(8,128)S(1)}, u32[]{:S(2)}, u32[]{:S(2)}) %collective-permute-start.3) | collective-permute-done | bytes 16416 | tf_op jit(solution)/shard_map/ppermute | solution.py:287
  31.0 0.6 %fusion = f32[1,32,128]{2,1,0:T(8,128)} fusion(f32[32,128]{1,0:T(8,128)S(1)} %collective-permute-done.3, f32[64,128]{1,0:T(8,128)S(1)} %slice_add_fusion), kind=kLoop, calls=%fused_computation.2 | loop fusion | flops 4096 | bytes 49152 | tf_op jit(solution)/shard_map/broadcast_in_dim | solution.py:287
  (4 shorter events, 0.0 us)
Async XLA Ops:
  1.9 15.2 %all-to-all-start = ((f32[16,16,128]{2,1,0:T(8,128)}), f32[16,16,128]{2,1,0:T(8,128)S(1)}, u32[]{:S(2)}, u32[]{:S(2)}) async-start(f32[16,16,128]{2,1,0:T(8,128)} %get-tuple-element.9), calls=%async_computation | async-start | bytes 262144 | tf_op jit(solution)/shard_map/all_to_all | solution.py:260
  9.1 5.9 %collective-permute-start = (f32[48,128]{1,0:T(8,128)S(1)}, f32[48,128]{1,0:T(8,128)S(1)}, u32[]{:S(2)}, u32[]{:S(2)}) collective-permute-start(f32[48,128]{1,0:T(8,128)S(1)} %get-tuple-element.8), channel_id=1, source_target_pairs={{0,65},{1,64},{2,67},{3,66},{4,69},{5,68},{6,71},{7,70},{8,73},{9,... | collective-permute-start | bytes 73736 | tf_op jit(solution)/shard_map/ppermute | solution.py:258
  19.4 6.4 %collective-permute-start.1 = (f32[128,128]{1,0:T(8,128)S(1)}, f32[128,128]{1,0:T(8,128)S(1)}, u32[]{:S(2)}, u32[]{:S(2)}) collective-permute-start(f32[128,128]{1,0:T(8,128)S(1)} %shard_map.74), channel_id=1, source_target_pairs={{0,65},{1,64},{2,67},{3,66},{4,69},{5,68},{6,71},{7,70},{8,73},{9,... | collective-permute-start | bytes 196616 | tf_op jit(solution)/shard_map/ppermute | solution.py:284
  25.9 1.3 %collective-permute-start.2 = (f32[64,128]{1,0:T(8,128)S(1)}, f32[64,128]{1,0:T(8,128)S(1)}, u32[]{:S(2)}, u32[]{:S(2)}) collective-permute-start(f32[64,128]{1,0:T(8,128)S(1)} %slice.17), channel_id=1, source_target_pairs={{0,32},{32,0},{64,96},{96,64},{1,33},{33,1},{65,97},{97,65},{2,34}... | collective-permute-start | bytes 98312 | tf_op jit(solution)/shard_map/ppermute | solution.py:286
  27.2 3.8 %collective-permute-start.3 = (f32[32,128]{1,0:T(8,128)S(1)}, f32[32,128]{1,0:T(8,128)S(1)}, u32[]{:S(2)}, u32[]{:S(2)}) collective-permute-start(f32[32,128]{1,0:T(8,128)S(1)} %slice.19), channel_id=1, source_target_pairs={{0,64},{32,96},{64,0},{96,32},{1,65},{33,97},{65,1},{97,33},{2,66}... | collective-permute-start | bytes 49160 | tf_op jit(solution)/shard_map/ppermute | solution.py:287

commit v5 on v4

--- a/solution.py
+++ b/solution.py
@@ -7,6 +7,7 @@
 from jax.experimental import pallas as pl
 from jax.experimental.pallas import tpu as pltpu
 from jax.sharding import PartitionSpec as P
+
 
 P_SIZE = 128
 IMG = 32768
@@ -197,19 +198,34 @@
     return values
 
 
-def image_kernel(scale, swap, note_ref, data_ref, image_ref, *scratch):
+def sum_blocks(note_ref, data_ref, scratch, sums, begin, end):
     buffers = (scratch[0:4], scratch[4:8])
-    steps = data_ref.shape[0] // 64
-    prepare(note_ref, data_ref, 0, 0, buffers[0])
+    prepare(note_ref, data_ref, begin, 0, buffers[0])
 
     def advance(step, sums):
         prepare(note_ref, data_ref, step, 1, buffers[1])
         sums = accumulate(buffers[0], sums)
-        prepare(note_ref, data_ref, (step + 1) & (steps - 1), 0, buffers[0])
+        prepare(note_ref, data_ref, jnp.minimum(step + 1, end - 1), 0, buffers[0])
         return accumulate(buffers[1], sums)
 
+    return lax.fori_loop(begin, end, advance, sums)
+
+
+def part_kernel(begin, end, note_ref, data_ref, even_ref, odd_ref, *scratch):
     zero = jnp.zeros((HALF, P_SIZE), jnp.float32)
-    even, odd = lax.fori_loop(0, steps, advance, (zero, zero))
+    even, odd = sum_blocks(note_ref, data_ref, scratch, (zero, zero), begin, end)
+    even_ref[...] = even
+    odd_ref[...] = odd
+
+
+def image_kernel(scale, swap, begin, end, note_ref, data_ref, *rest):
+    if begin:
+        even_ref, odd_ref, *rest = rest
+        sums = (even_ref[...], odd_ref[...])
+    else:
+        sums = (jnp.zeros((HALF, P_SIZE), jnp.float32),) * 2
+    keep_ref, send_ref, image_ref, *scratch = rest
+    even, odd = sum_blocks(note_ref, data_ref, scratch, sums, begin, end)
     even, odd = even * scale, odd * scale
     core = lax.axis_index("freq") & 1
     far = (lax.axis_index("freq") >> 1) ^ swap
@@ -233,6 +249,8 @@
             slot = ((piece & 1) ^ core) * 2 + ((piece >> 1) ^ far)
             place = pl.multiple_of(slot * 32 + 8 * (index % 4), 8)
             image_ref[pl.ds(place, 8), :] = values
+    keep_ref[...] = image_ref[0:HALF, :]
+    send_ref[...] = image_ref[HALF:, :]
 
 
 SMALL = pltpu.CompilerParams(vmem_limit_bytes=8 << 20)
@@ -266,24 +284,40 @@
         pltpu.VMEM((8, 8, LANES), jnp.float32),
     ]
     scratch = buffers * 2
-    cost = pl.CostEstimate(
-        flops=2 * 2 * HALF * P_SIZE * 2 * plane * KEEP, bytes_accessed=1 << 18, transcendentals=0
-    )
-
-    def image(swap, note):
+    scale = 2.0 / math.sqrt(total)
+    steps = plane // 4
+    rows = jax.ShapeDtypeStruct((HALF, P_SIZE), jnp.float32)
+
+    def call(kernel, count, operands, scratch):
+        cost = pl.CostEstimate(
+            flops=count * 2 * 2 * HALF * P_SIZE * 16 * KEEP, bytes_accessed=1 << 18, transcendentals=0
+        )
         return pl.pallas_call(
-            functools.partial(image_kernel, 2.0 / math.sqrt(total), swap),
-            out_shape=jax.ShapeDtypeStruct((P_SIZE, P_SIZE), jnp.float32),
-            in_specs=[VMEM] * 2,
-            out_specs=VMEM,
+            kernel,
+            out_shape=(rows, rows),
+            in_specs=[VMEM] * len(operands),
+            out_specs=(VMEM, VMEM),
             scratch_shapes=scratch,
             compiler_params=SMALL,
             cost_estimate=cost,
-        )(note, near)
-
-    joined = lax.ppermute(image(1, other), ("freq", "facet"), across)
-    joined = joined + image(0, mine)
-    half = joined[:HALF] + lax.ppermute(joined[HALF:], "freq", [(i, i ^ 1) for i in range(4)])
+        )(*operands)
+
+    whole = [pltpu.VMEM((P_SIZE, P_SIZE), jnp.float32)]
+    cores = [(i, i ^ 1) for i in range(4)]
+    keep, send = call(
+        functools.partial(image_kernel, scale, 1, 0, steps), steps, (other, near), whole + scratch
+    )
+    middle = steps // 2
+    sums = call(functools.partial(part_kernel, 0, middle), middle, (mine, near), scratch)
+    visitor, sums = lax.optimization_barrier(
+        (keep + lax.ppermute(send, "freq", cores), tuple(sums))
+    )
+    visitor = lax.ppermute(visitor, ("freq", "facet"), across)
+    keep, send = call(
+        functools.partial(image_kernel, scale, 0, middle, steps),
+        steps - middle, (mine, near, *sums), whole + scratch,
+    )
+    half = keep + lax.ppermute(send, "freq", cores) + visitor
     return (half[:32] + lax.ppermute(half[32:], "freq", [(i, i ^ 2) for i in range(4)]))[None]
 
 

time: 31.8 us -> 33.1 us (1.041)
  waiting for transfers between devices: 8.79 us -> 9.55 us
  starting transfers between devices: 15.6 us -> 16 us
    ppermute x2 -> x3, waiting for transfers between devices: 1.2 us -> 1.95 us  [the longest x1 1.89 us: body(): visitor = lax.ppermute(visitor, ('freq', 'facet'), across)]
    ppermute x2 -> x3, starting transfers between devices: 4.2 us -> 4.66 us  [the longest x1 4.04 us: body(): visitor = lax.ppermute(visitor, ('freq', 'facet'), across)]
    pallas_call x2 -> x3, Pallas kernels: 4.64 us -> 4.73 us  [call(): pl.pallas_call(kernel, out_shape=(rows, rows), in_specs=[VMEM] * len(oper...]
  transfers between devices with their start and end apart: 5 -> 6, of which waited for: 4 -> 5; matrix products, arithmetic and copies ran while one was open for 0% -> 0% of each run, Pallas kernels for 7% -> 3%
where the time goes in v5:
time: 33.1 us; the launch traced here: 32.9 us
  starting transfers between devices  16 us (48%)
  waiting for transfers between devices  9.55 us (29%)
  Pallas kernels  6.63 us (20%)
  other arithmetic  0.62 us (2%)
    all_to_all x1, starting transfers between devices, body(): near = lax.all_to_all(packed, 'facet', 0, 0, axis_index_groups=groups)  7.16 us
    pallas_call x3, Pallas kernels, call(): pl.pallas_call(kernel, out_shape=(rows, rows), in_specs=[VMEM] * len(oper...  4.73 us
    ppermute x1, starting transfers between devices, body(): other = lax.ppermute(other, ('freq', 'facet'), across)  4.12 us
    ppermute x1, starting transfers between devices, body(): visitor = lax.ppermute(visitor, ('freq', 'facet'), across)  4.04 us
    ppermute x1, waiting for transfers between devices, body(): lax.ppermute(half[32:], 'freq', [(i, i ^ 2) for i in range(4)])  3.73 us
    all_to_all x1, waiting for transfers between devices, body(): near = lax.all_to_all(packed, 'facet', 0, 0, axis_index_groups=groups)  2.06 us
    pallas_call x1, Pallas kernels, body(): pl.pallas_call(pack_kernel, out_shape=(jax.ShapeDtypeStruct((plane, 16, L...  1.9 us
    ppermute x1, waiting for transfers between devices, body(): visitor = lax.ppermute(visitor, ('freq', 'facet'), across)  1.89 us
  transfers between devices with their start and end apart: 6, of which 5 were waited for; matrix products, arithmetic and copies ran while one was open for 0% of the time, Pallas kernels for 3%

profile of v5, /device:TPU:0, one launch (start us, length us, event | category | flops | bytes accessed | tf_op | source)
XLA Modules:
  0.0 32.9 jit_solution(5399793005155352736)
XLA Ops:
  0.0 1.9 %shard_map.73 = (f32[16,16,128]{2,1,0:T(8,128)}, f32[48,128]{1,0:T(8,128)S(1)}, f32[48,128]{1,0:T(8,128)S(1)}) custom-call(f32[2,2,512]{2,1,0:T(2,128)} %vis_in.1, f32[2,512]{1,0:T(2,128)} %weight_in.1, s32[2,2,512]{2,1,0:T(2,128)} %uv_in.1, s32[2,512]{1,0:T(2,128)} %flag_in.1, s32[1,64]{1,0:T(1,128)} %bitcast.7, f32[1,64]{1,0:T(1,128)} %beam_in.1, ...), custom_call_target="tpu_custom_call" | custom-call | tf_op jit(solution)/shard_map/pallas_call | solution.py:263
  1.9 7.2 %all-to-all-start = ((f32[16,16,128]{2,1,0:T(8,128)}), f32[16,16,128]{2,1,0:T(8,128)S(1)}, u32[]{:S(2)}, u32[]{:S(2)}) async-start(f32[16,16,128]{2,1,0:T(8,128)} %get-tuple-element.18), calls=%async_computation | async-start | bytes 262144 | tf_op jit(solution)/shard_map/all_to_all | solution.py:278
  9.1 4.1 %collective-permute-start = (f32[48,128]{1,0:T(8,128)S(1)}, f32[48,128]{1,0:T(8,128)S(1)}, u32[]{:S(2)}, u32[]{:S(2)}) collective-permute-start(f32[48,128]{1,0:T(8,128)S(1)} %get-tuple-element.19), channel_id=1, source_target_pairs={{0,65},{1,64},{2,67},{3,66},{4,69},{5,68},{6,71},{7,70},{8,73},{9,... | collective-permute-start | bytes 73736 | tf_op jit(solution)/shard_map/ppermute | solution.py:276
  13.2 1.8 %collective-permute-done.note_ref = f32[48,128]{1,0:T(8,128)S(1)} collective-permute-done((f32[48,128]{1,0:T(8,128)S(1)}, f32[48,128]{1,0:T(8,128)S(1)}, u32[]{:S(2)}, u32[]{:S(2)}) %collective-permute-start) | collective-permute-done | bytes 24608 | tf_op jit(solution)/shard_map/ppermute | solution.py:276
  15.0 2.1 %all-to-all-done = f32[16,16,128]{2,1,0:T(8,128)S(1)} async-done(((f32[16,16,128]{2,1,0:T(8,128)}), f32[16,16,128]{2,1,0:T(8,128)S(1)}, u32[]{:S(2)}, u32[]{:S(2)}) %all-to-all-start) | async-done | bytes 131104 | tf_op jit(solution)/shard_map/all_to_all | solution.py:278
  17.1 2.3 %shard_map.74 = (f32[64,128]{1,0:T(8,128)S(1)}, f32[64,128]{1,0:T(8,128)S(1)}) custom-call(f32[48,128]{1,0:T(8,128)S(1)} %collective-permute-done.note_ref, f32[256,128]{1,0:T(8,128)S(1)} %bitcast.4), custom_call_target="tpu_custom_call" | custom-call | flops 536870912 | bytes 262144 | tf_op jit(solution)/shard_map/pallas_call | solution.py:295
  19.4 0.1 collective-permute-start.1
  19.5 1.1 %shard_map.75 = (f32[64,128]{1,0:T(8,128)S(1)}, f32[64,128]{1,0:T(8,128)S(1)}) custom-call(f32[48,128]{1,0:T(8,128)S(1)} %get-tuple-element.17.note_ref, f32[256,128]{1,0:T(8,128)S(1)} %bitcast.5), custom_call_target="tpu_custom_call" | custom-call | flops 268435456 | bytes 262144 | tf_op jit(solution)/shard_map/pallas_call | solution.py:295
  20.6 0.1 collective-permute-done.1
  20.7 1.3 %shard_map.76 = (f32[64,128]{1,0:T(8,128)S(1)}, f32[64,128]{1,0:T(8,128)S(1)}) custom-call(f32[48,128]{1,0:T(8,128)S(1)} %get-tuple-element.17.note_ref, f32[256,128]{1,0:T(8,128)S(1)} %bitcast.6, f32[64,128]{1,0:T(8,128)S(1)} %get-tuple-element.24.rest_0_, f32[64,128]{1,0:T(8,128)S(1)} %get-tuple-element.25.rest_1_), custom_call_target="tpu_custom_call" | custom-call | flops 268435456 | bytes 262144 | tf_op jit(solution)/shard_map/pallas_call | solution.py:295
  22.0 0.5 %collective-permute-start.2 = (f32[64,128]{1,0:T(8,128)S(1)}, f32[64,128]{1,0:T(8,128)S(1)}, u32[]{:S(2)}, u32[]{:S(2)}) collective-permute-start(f32[64,128]{1,0:T(8,128)S(1)} %get-tuple-element.27), channel_id=1, source_target_pairs={{0,32},{32,0},{64,96},{96,64},{1,33},{33,1},{65,97},{97,65},{2,34}... | collective-permute-start | bytes 98312 | tf_op jit(solution)/shard_map/ppermute | solution.py:320
  22.5 4.0 %collective-permute-start.3 = (f32[64,128]{1,0:T(8,128)S(1)}, f32[64,128]{1,0:T(8,128)S(1)}, u32[]{:S(2)}, u32[]{:S(2)}) collective-permute-start(f32[64,128]{1,0:T(8,128)S(1)} %add.12), channel_id=1, source_target_pairs={{0,65},{1,64},{2,67},{3,66},{4,69},{5,68},{6,71},{7,70},{8,73},{9,... | collective-permute-start | bytes 98312 | tf_op jit(solution)/shard_map/ppermute | solution.py:315
  26.5 0.0 collective-permute-done.2
  26.5 1.9 %collective-permute-done.3 = f32[64,128]{1,0:T(8,128)S(1)} collective-permute-done((f32[64,128]{1,0:T(8,128)S(1)}, f32[64,128]{1,0:T(8,128)S(1)}, u32[]{:S(2)}, u32[]{:S(2)}) %collective-permute-start.3) | collective-permute-done | bytes 32800 | tf_op jit(solution)/shard_map/ppermute | solution.py:315
  28.4 0.1 collective-permute-start.4
  28.5 3.7 %collective-permute-done.4 = f32[32,128]{1,0:T(8,128)S(1)} collective-permute-done((f32[32,128]{1,0:T(8,128)S(1)}, f32[32,128]{1,0:T(8,128)S(1)}, u32[]{:S(2)}, u32[]{:S(2)}) %collective-permute-start.4) | collective-permute-done | bytes 16416 | tf_op jit(solution)/shard_map/ppermute | solution.py:321
  32.3 0.6 %fusion = f32[1,32,128]{2,1,0:T(8,128)} fusion(f32[32,128]{1,0:T(8,128)S(1)} %collective-permute-done.4, f32[64,128]{1,0:T(8,128)S(1)} %add_add_fusion), kind=kLoop, calls=%fused_computation.2 | loop fusion | flops 4096 | bytes 49152 | tf_op jit(solution)/shard_map/broadcast_in_dim | solution.py:321
  (3 shorter events, 0.0 us)
Async XLA Ops:
  1.9 15.2 %all-to-all-start = ((f32[16,16,128]{2,1,0:T(8,128)}), f32[16,16,128]{2,1,0:T(8,128)S(1)}, u32[]{:S(2)}, u32[]{:S(2)}) async-start(f32[16,16,128]{2,1,0:T(8,128)} %get-tuple-element.18), calls=%async_computation | async-start | bytes 262144 | tf_op jit(solution)/shard_map/all_to_all | solution.py:278
  9.1 5.9 %collective-permute-start = (f32[48,128]{1,0:T(8,128)S(1)}, f32[48,128]{1,0:T(8,128)S(1)}, u32[]{:S(2)}, u32[]{:S(2)}) collective-permute-start(f32[48,128]{1,0:T(8,128)S(1)} %get-tuple-element.19), channel_id=1, source_target_pairs={{0,65},{1,64},{2,67},{3,66},{4,69},{5,68},{6,71},{7,70},{8,73},{9,... | collective-permute-start | bytes 73736 | tf_op jit(solution)/shard_map/ppermute | solution.py:276
  19.4 1.3 %collective-permute-start.1 = (f32[64,128]{1,0:T(8,128)S(1)}, f32[64,128]{1,0:T(8,128)S(1)}, u32[]{:S(2)}, u32[]{:S(2)}) collective-permute-start(f32[64,128]{1,0:T(8,128)S(1)} %get-tuple-element.21), channel_id=1, source_target_pairs={{0,32},{32,0},{64,96},{96,64},{1,33},{33,1},{65,97},{97,65},{2,34}... | collective-permute-start | bytes 98312 | tf_op jit(solution)/shard_map/ppermute | solution.py:313
  22.0 4.6 %collective-permute-start.2 = (f32[64,128]{1,0:T(8,128)S(1)}, f32[64,128]{1,0:T(8,128)S(1)}, u32[]{:S(2)}, u32[]{:S(2)}) collective-permute-start(f32[64,128]{1,0:T(8,128)S(1)} %get-tuple-element.27), channel_id=1, source_target_pairs={{0,32},{32,0},{64,96},{96,64},{1,33},{33,1},{65,97},{97,65},{2,34}... | collective-permute-start | bytes 98312 | tf_op jit(solution)/shard_map/ppermute | solution.py:320
  22.5 5.9 %collective-permute-start.3 = (f32[64,128]{1,0:T(8,128)S(1)}, f32[64,128]{1,0:T(8,128)S(1)}, u32[]{:S(2)}, u32[]{:S(2)}) collective-permute-start(f32[64,128]{1,0:T(8,128)S(1)} %add.12), channel_id=1, source_target_pairs={{0,65},{1,64},{2,67},{3,66},{4,69},{5,68},{6,71},{7,70},{8,73},{9,... | collective-permute-start | bytes 98312 | tf_op jit(solution)/shard_map/ppermute | solution.py:315
  28.4 3.8 %collective-permute-start.4 = (f32[32,128]{1,0:T(8,128)S(1)}, f32[32,128]{1,0:T(8,128)S(1)}, u32[]{:S(2)}, u32[]{:S(2)}) collective-permute-start(f32[32,128]{1,0:T(8,128)S(1)} %slice.9), channel_id=1, source_target_pairs={{0,64},{32,96},{64,0},{96,32},{1,65},{33,97},{65,1},{97,33},{2,66}... | collective-permute-start | bytes 49160 | tf_op jit(solution)/shard_map/ppermute | solution.py:321

commit v6 on v4

--- a/solution.py
+++ b/solution.py
@@ -129,25 +129,17 @@
     )
 
 
-def prepare(note_ref, data_ref, step, half, buffers):
-    fine_v, fine_u, outer, coarse = buffers
-    column = note_ref[0:8, :].astype(jnp.int32)
-    row = note_ref[8:16, :].astype(jnp.int32)
+def prepare(notes, data_ref, step, half, buffers):
+    fine_v, fine_u, coarse, *outers = buffers
     tile = step >> 1
     member = step & 1
-    place = 16 + member * (data_ref.shape[0] // 16) + tile * 8
-    gain = note_ref[pl.ds(pl.multiple_of(place, 8), 8), :]
+    place = pl.multiple_of(16 + member * (data_ref.shape[0] // 16) + tile * 8, 8)
     first = tile * 128 + 8 * half + member
     real, imag, u, v = (
         data_ref[pl.ds(first + 2 * kind, 8, stride=16), :] for kind in range(4)
     )
     u = u.astype(jnp.int32)
     v = v.astype(jnp.int32)
-    real = real * gain
-    imag = imag * gain
-    sine, cosine = sine_cosine(u * column + v * row)
-    centre_real = real * cosine - imag * sine
-    centre_imag = real * sine + imag * cosine
     near_v = sine_cosine(v)
     near_u = sine_cosine(u)
     for near, fine in ((near_v, fine_v), (near_u, fine_u)):
@@ -163,25 +155,35 @@
         coarse[2 * far] = cosines[far]
         coarse[2 * far + 1] = sines[far]
     sines, cosines = half_steps(*near_v, 4)
-    for far in range(4):
-        rc, isn = centre_real * cosines[far], centre_imag * sines[far]
-        ic, rs = centre_imag * cosines[far], centre_real * sines[far]
-        above, below = 4 + far, 3 - far
-        outer[2 * above] = rc - isn
-        outer[2 * above + 1] = ic + rs
-        outer[2 * below] = rc + isn
-        outer[2 * below + 1] = ic - rs
+    for note_ref, outer in zip(notes, outers):
+        column = note_ref[0:8, :].astype(jnp.int32)
+        row = note_ref[8:16, :].astype(jnp.int32)
+        gain = note_ref[pl.ds(place, 8), :]
+        sine, cosine = sine_cosine(u * column + v * row)
+        sine, cosine = sine * gain, cosine * gain
+        centre_real = real * cosine - imag * sine
+        centre_imag = real * sine + imag * cosine
+        for far in range(4):
+            rc, isn = centre_real * cosines[far], centre_imag * sines[far]
+            ic, rs = centre_imag * cosines[far], centre_real * sines[far]
+            above, below = 4 + far, 3 - far
+            outer[2 * above] = rc - isn
+            outer[2 * above + 1] = ic + rs
+            outer[2 * below] = rc + isn
+            outer[2 * below + 1] = ic - rs
 
 
 def accumulate(buffers, sums):
-    fine_v, fine_u, outer, coarse = buffers
+    fine_v, fine_u, coarse, *outers = buffers
     even, odd = sums
     for pair in range(4):
-        tables = [
-            chunk_tables(coarse, fine_u, 4, chunk) + chunk_tables(outer, fine_v, 8, chunk)
-            for chunk in (2 * pair, 2 * pair + 1)
-        ]
-        c, s, a, b = (jnp.concatenate(table, axis=1) for table in zip(*tables))
+        left, right = [], []
+        for chunk in (2 * pair, 2 * pair + 1):
+            left.append(chunk_tables(coarse, fine_u, 4, chunk))
+            facets = [chunk_tables(outer, fine_v, 8, chunk) for outer in outers]
+            right.append(tuple(jnp.concatenate(table, axis=0) for table in zip(*facets)))
+        c, s = (jnp.concatenate(table, axis=1) for table in zip(*left))
+        a, b = (jnp.concatenate(table, axis=1) for table in zip(*right))
         contract = (((1,), (1,)), ((), ()))
         even = even + lax.dot_general(c, a, contract, preferred_element_type=jnp.float32)
         odd = odd + lax.dot_general(s, b, contract, preferred_element_type=jnp.float32)
@@ -197,42 +199,47 @@
     return values
 
 
-def image_kernel(scale, swap, note_ref, data_ref, image_ref, *scratch):
-    buffers = (scratch[0:4], scratch[4:8])
+def image_kernel(scale, mine_ref, other_ref, data_ref, keep_ref, send_ref, image_ref, *scratch):
+    notes = (mine_ref, other_ref)
+    buffers = (scratch[0:5], scratch[5:10])
     steps = data_ref.shape[0] // 64
-    prepare(note_ref, data_ref, 0, 0, buffers[0])
+    prepare(notes, data_ref, 0, 0, buffers[0])
 
     def advance(step, sums):
-        prepare(note_ref, data_ref, step, 1, buffers[1])
+        prepare(notes, data_ref, step, 1, buffers[1])
         sums = accumulate(buffers[0], sums)
-        prepare(note_ref, data_ref, (step + 1) & (steps - 1), 0, buffers[0])
+        prepare(notes, data_ref, (step + 1) & (steps - 1), 0, buffers[0])
         return accumulate(buffers[1], sums)
 
-    zero = jnp.zeros((HALF, P_SIZE), jnp.float32)
-    even, odd = lax.fori_loop(0, steps, advance, (zero, zero))
-    even, odd = even * scale, odd * scale
+    zero = jnp.zeros((HALF, 2 * P_SIZE), jnp.float32)
+    evens, odds = lax.fori_loop(0, steps, advance, (zero, zero))
     core = lax.axis_index("freq") & 1
-    far = (lax.axis_index("freq") >> 1) ^ swap
+    far = lax.axis_index("freq") >> 1
     lane = lax.broadcasted_iota(jnp.int32, (8, P_SIZE), 1)
     near = jnp.where((lane & 8) == 8, lane ^ 8, lane ^ 7)
-    sign = jnp.where((lane & 8) == 8, -1.0, 1.0)
-    for block in range(8):
-        base = 16 * (block // 2)
-        above = block % 2 == 1
-        even_p, even_q = even[base : base + 8], even[base + 8 : base + 16]
-        odd_p, odd_q = odd[base : base + 8], odd[base + 8 : base + 16]
-        even_row = even_p - even_q if above else even_p + even_q
-        odd_row = odd_p + odd_q if above else odd_p - odd_q
-        less, more = even_row - odd_row, even_row + odd_row
-        for index, one, two, reverse in (
-            (8 + block, less, more, not above),
-            (7 - block, more, less, above),
-        ):
-            values = paired(one, near, reverse) + sign * paired(two, near ^ 8, reverse)
-            piece = index // 4
-            slot = ((piece & 1) ^ core) * 2 + ((piece >> 1) ^ far)
-            place = pl.multiple_of(slot * 32 + 8 * (index % 4), 8)
-            image_ref[pl.ds(place, 8), :] = values
+    sign = jnp.where((lane & 8) == 8, -scale, scale)
+    for facet in range(2):
+        columns = slice(facet * P_SIZE, (facet + 1) * P_SIZE)
+        even, odd = evens[:, columns], odds[:, columns]
+        for block in range(8):
+            base = 16 * (block // 2)
+            above = block % 2 == 1
+            even_p, even_q = even[base : base + 8], even[base + 8 : base + 16]
+            odd_p, odd_q = odd[base : base + 8], odd[base + 8 : base + 16]
+            even_row = even_p - even_q if above else even_p + even_q
+            odd_row = odd_p + odd_q if above else odd_p - odd_q
+            less, more = even_row - odd_row, even_row + odd_row
+            for index, one, two, reverse in (
+                (8 + block, less, more, not above),
+                (7 - block, more, less, above),
+            ):
+                values = scale * paired(one, near, reverse) + sign * paired(two, near ^ 8, reverse)
+                piece = index // 4
+                slot = ((piece & 1) ^ core) * 4 + 2 * facet + ((piece >> 1) ^ far)
+                place = pl.multiple_of(slot * 32 + 8 * (index % 4), 8)
+                image_ref[pl.ds(place, 8), :] = values
+    keep_ref[...] = image_ref[0:P_SIZE, :]
+    send_ref[...] = image_ref[P_SIZE:, :]
 
 
 SMALL = pltpu.CompilerParams(vmem_limit_bytes=8 << 20)
@@ -259,32 +266,32 @@
     groups = [list(range(side, 2 * plane, 2)) for side in range(2)]
     near = lax.all_to_all(packed, "facet", 0, 0, axis_index_groups=groups)
     near = near.reshape(plane * 16, LANES)
+    outer = pltpu.VMEM((16, 8, LANES), jnp.float32)
     buffers = [
         pltpu.VMEM((2, 64, LANES), jnp.float32),
         pltpu.VMEM((2, 64, LANES), jnp.float32),
-        pltpu.VMEM((16, 8, LANES), jnp.float32),
         pltpu.VMEM((8, 8, LANES), jnp.float32),
+        outer,
+        outer,
     ]
-    scratch = buffers * 2
-    cost = pl.CostEstimate(
-        flops=2 * 2 * HALF * P_SIZE * 2 * plane * KEEP, bytes_accessed=1 << 18, transcendentals=0
-    )
-
-    def image(swap, note):
-        return pl.pallas_call(
-            functools.partial(image_kernel, 2.0 / math.sqrt(total), swap),
-            out_shape=jax.ShapeDtypeStruct((P_SIZE, P_SIZE), jnp.float32),
-            in_specs=[VMEM] * 2,
-            out_specs=VMEM,
-            scratch_shapes=scratch,
-            compiler_params=SMALL,
-            cost_estimate=cost,
-        )(note, near)
-
-    joined = lax.ppermute(image(1, other), ("freq", "facet"), across)
-    joined = joined + image(0, mine)
-    half = joined[:HALF] + lax.ppermute(joined[HALF:], "freq", [(i, i ^ 1) for i in range(4)])
-    return (half[:32] + lax.ppermute(half[32:], "freq", [(i, i ^ 2) for i in range(4)]))[None]
+    image = jax.ShapeDtypeStruct((P_SIZE, P_SIZE), jnp.float32)
+    keep, send = pl.pallas_call(
+        functools.partial(image_kernel, 2.0 / math.sqrt(total)),
+        out_shape=(image, image),
+        in_specs=[VMEM] * 3,
+        out_specs=(VMEM, VMEM),
+        scratch_shapes=[pltpu.VMEM((2 * P_SIZE, P_SIZE), jnp.float32)] + buffers * 2,
+        compiler_params=SMALL,
+    )(mine, other, near)
+    half = keep + lax.ppermute(send, "freq", [(i, i ^ 1) for i in range(4)])
+    result = half[:32]
+    for piece, partner in ((2, 1), (1, 64), (3, 65)):
+        result = result + lax.ppermute(
+            half[32 * piece : 32 * piece + 32],
+            ("freq", "facet"),
+            [(i, i ^ partner) for i in range(8 * plane)],
+        )
+    return result[None]
 
 
 def solution(mesh):

time: 31.8 us -> 31.6 us (level)
  Pallas kernels: 6.55 us -> 5.35 us
  starting transfers between devices: 15.6 us -> 16.3 us
    pallas_call x2 -> x1, Pallas kernels: 4.64 us -> 3.45 us  [body(): pl.pallas_call(functools.partial(image_kernel, 2.0 / math.sqrt(total)), o...]
    ppermute x3 -> x4, starting transfers between devices: 4.29 us -> 5.06 us  [the longest x3 4.97 us: body(): lax.ppermute(half[32 * piece:32 * piece + 32], ('freq', 'facet'), [(i, i...]
    ppermute x3 -> x4, waiting for transfers between devices: 4.92 us -> 5.17 us  [the longest x3 3.93 us: body(): lax.ppermute(half[32 * piece:32 * piece + 32], ('freq', 'facet'), [(i, i...]
  transfers between devices with their start and end apart: 5 -> 6, of which waited for: 4 -> 5; matrix products, arithmetic and copies ran while one was open for 0% -> 0% of each run, Pallas kernels for 7% -> 0%
where the time goes in v6:
time: 31.6 us; the launch traced here: 31.4 us
  starting transfers between devices  16.3 us (52%)
  waiting for transfers between devices  9.04 us (29%)
  Pallas kernels  5.35 us (17%)
  other arithmetic  0.62 us (2%)
    all_to_all x1, starting transfers between devices, body(): near = lax.all_to_all(packed, 'facet', 0, 0, axis_index_groups=groups)  7.16 us
    ppermute x3, starting transfers between devices, body(): lax.ppermute(half[32 * piece:32 * piece + 32], ('freq', 'facet'), [(i, i...  4.97 us
    ppermute x1, starting transfers between devices, body(): other = lax.ppermute(other, ('freq', 'facet'), across)  4.12 us
    ppermute x3, waiting for transfers between devices, body(): lax.ppermute(half[32 * piece:32 * piece + 32], ('freq', 'facet'), [(i, i...  3.93 us
    pallas_call x1, Pallas kernels, body(): pl.pallas_call(functools.partial(image_kernel, 2.0 / math.sqrt(total)), o...  3.45 us
    all_to_all x1, waiting for transfers between devices, body(): near = lax.all_to_all(packed, 'facet', 0, 0, axis_index_groups=groups)  2.06 us
    pallas_call x1, Pallas kernels, body(): pl.pallas_call(pack_kernel, out_shape=(jax.ShapeDtypeStruct((plane, 16, L...  1.91 us
    ppermute x1, waiting for transfers between devices, body(): other = lax.ppermute(other, ('freq', 'facet'), across)  1.81 us
  transfers between devices with their start and end apart: 6, of which 5 were waited for; matrix products, arithmetic and copies ran while one was open for 0% of the time, Pallas kernels for 0%

profile of v6, /device:TPU:0, one launch (start us, length us, event | category | flops | bytes accessed | tf_op | source)
XLA Modules:
  0.0 31.4 jit_solution(18406214684558704211)
XLA Ops:
  0.0 1.9 %shard_map.73 = (f32[16,16,128]{2,1,0:T(8,128)}, f32[48,128]{1,0:T(8,128)S(1)}, f32[48,128]{1,0:T(8,128)S(1)}) custom-call(f32[2,2,512]{2,1,0:T(2,128)} %vis_in.1, f32[2,512]{1,0:T(2,128)} %weight_in.1, s32[2,2,512]{2,1,0:T(2,128)} %uv_in.1, s32[2,512]{1,0:T(2,128)} %flag_in.1, s32[1,64]{1,0:T(1,128)} %bitcast.5, f32[1,64]{1,0:T(1,128)} %beam_in.1, ...), custom_call_target="tpu_custom_call" | custom-call | tf_op jit(solution)/shard_map/pallas_call | solution.py:252
  1.9 7.2 %all-to-all-start = ((f32[16,16,128]{2,1,0:T(8,128)}), f32[16,16,128]{2,1,0:T(8,128)S(1)}, u32[]{:S(2)}, u32[]{:S(2)}) async-start(f32[16,16,128]{2,1,0:T(8,128)} %get-tuple-element.12), calls=%async_computation | async-start | bytes 262144 | tf_op jit(solution)/shard_map/all_to_all | solution.py:267
  9.1 4.1 %collective-permute-start = (f32[48,128]{1,0:T(8,128)S(1)}, f32[48,128]{1,0:T(8,128)S(1)}, u32[]{:S(2)}, u32[]{:S(2)}) collective-permute-start(f32[48,128]{1,0:T(8,128)S(1)} %get-tuple-element.11), channel_id=1, source_target_pairs={{0,65},{1,64},{2,67},{3,66},{4,69},{5,68},{6,71},{7,70},{8,73},{9,... | collective-permute-start | bytes 73736 | tf_op jit(solution)/shard_map/ppermute | solution.py:265
  13.2 1.8 %collective-permute-done.other_ref = f32[48,128]{1,0:T(8,128)S(1)} collective-permute-done((f32[48,128]{1,0:T(8,128)S(1)}, f32[48,128]{1,0:T(8,128)S(1)}, u32[]{:S(2)}, u32[]{:S(2)}) %collective-permute-start) | collective-permute-done | bytes 24608 | tf_op jit(solution)/shard_map/ppermute | solution.py:265
  15.0 2.1 %all-to-all-done = f32[16,16,128]{2,1,0:T(8,128)S(1)} async-done(((f32[16,16,128]{2,1,0:T(8,128)}), f32[16,16,128]{2,1,0:T(8,128)S(1)}, u32[]{:S(2)}, u32[]{:S(2)}) %all-to-all-start) | async-done | bytes 131104 | tf_op jit(solution)/shard_map/all_to_all | solution.py:267
  17.1 3.4 %shard_map.74 = (f32[128,128]{1,0:T(8,128)S(1)}, f32[128,128]{1,0:T(8,128)S(1)}) custom-call(f32[48,128]{1,0:T(8,128)S(1)} %get-tuple-element.10.mine_ref, f32[48,128]{1,0:T(8,128)S(1)} %collective-permute-done.other_ref, f32[256,128]{1,0:T(8,128)S(1)} %bitcast.4), custom_call_target="tpu_custom_call" | custom-call | tf_op jit(solution)/shard_map/pallas_call | solution.py:278
  20.5 0.1 collective-permute-start.1
  20.6 1.2 %collective-permute-done.1 = f32[128,128]{1,0:T(8,128)S(1)} collective-permute-done((f32[128,128]{1,0:T(8,128)S(1)}, f32[128,128]{1,0:T(8,128)S(1)}, u32[]{:S(2)}, u32[]{:S(2)}) %collective-permute-start.1) | collective-permute-done | bytes 65568 | tf_op jit(solution)/shard_map/ppermute | solution.py:286
  21.9 4.0 %collective-permute-start.2 = (f32[32,128]{1,0:T(8,128)S(1)}, f32[32,128]{1,0:T(8,128)S(1)}, u32[]{:S(2)}, u32[]{:S(2)}) collective-permute-start(f32[32,128]{1,0:T(8,128)S(1)} %get-tuple-element.15), channel_id=1, source_target_pairs={{0,1},{1,0},{2,3},{3,2},{4,5},{5,4},{6,7},{7,6},{8,9},{9,8},{10,11... | collective-permute-start | bytes 49160 | tf_op jit(solution)/shard_map/ppermute | solution.py:289
  25.8 0.7 %collective-permute-start.4 = (f32[32,128]{1,0:T(8,128)S(1)}, f32[32,128]{1,0:T(8,128)S(1)}, u32[]{:S(2)}, u32[]{:S(2)}) collective-permute-start(f32[32,128]{1,0:T(8,128)S(1)} %get-tuple-element.16), channel_id=1, source_target_pairs={{0,65},{1,64},{2,67},{3,66},{4,69},{5,68},{6,71},{7,70},{8,73},{9,... | collective-permute-start | bytes 49160 | tf_op jit(solution)/shard_map/ppermute | solution.py:289
  26.6 0.3 collective-permute-start.3
  26.9 0.7 %collective-permute-done.2 = f32[32,128]{1,0:T(8,128)S(1)} collective-permute-done((f32[32,128]{1,0:T(8,128)S(1)}, f32[32,128]{1,0:T(8,128)S(1)}, u32[]{:S(2)}, u32[]{:S(2)}) %collective-permute-start.2) | collective-permute-done | bytes 16416 | tf_op jit(solution)/shard_map/ppermute | solution.py:289
  27.6 3.2 %collective-permute-done.4 = f32[32,128]{1,0:T(8,128)S(1)} collective-permute-done((f32[32,128]{1,0:T(8,128)S(1)}, f32[32,128]{1,0:T(8,128)S(1)}, u32[]{:S(2)}, u32[]{:S(2)}) %collective-permute-start.4) | collective-permute-done | bytes 16416 | tf_op jit(solution)/shard_map/ppermute | solution.py:289
  30.8 0.0 collective-permute-done.3
  30.8 0.6 %fusion.2 = f32[1,32,128]{2,1,0:T(8,128)} fusion(f32[32,128]{1,0:T(8,128)S(1)} %collective-permute-done.4, f32[32,128]{1,0:T(8,128)S(1)} %collective-permute-done.3, f32[32,128]{1,0:T(8,128)S(1)} %collective-permute-done.2, f32[128,128]{1,0:T(8,128)S(1)} %add.12), kind=kLoop, calls=%fused_computation.3 | loop fusion | flops 12288 | bytes 81920 | tf_op jit(solution)/shard_map/broadcast_in_dim | solution.py:294
  (2 shorter events, 0.0 us)
Async XLA Ops:
  1.9 15.2 %all-to-all-start = ((f32[16,16,128]{2,1,0:T(8,128)}), f32[16,16,128]{2,1,0:T(8,128)S(1)}, u32[]{:S(2)}, u32[]{:S(2)}) async-start(f32[16,16,128]{2,1,0:T(8,128)} %get-tuple-element.12), calls=%async_computation | async-start | bytes 262144 | tf_op jit(solution)/shard_map/all_to_all | solution.py:267
  9.1 5.9 %collective-permute-start = (f32[48,128]{1,0:T(8,128)S(1)}, f32[48,128]{1,0:T(8,128)S(1)}, u32[]{:S(2)}, u32[]{:S(2)}) collective-permute-start(f32[48,128]{1,0:T(8,128)S(1)} %get-tuple-element.11), channel_id=1, source_target_pairs={{0,65},{1,64},{2,67},{3,66},{4,69},{5,68},{6,71},{7,70},{8,73},{9,... | collective-permute-start | bytes 73736 | tf_op jit(solution)/shard_map/ppermute | solution.py:265
  20.5 1.3 %collective-permute-start.1 = (f32[128,128]{1,0:T(8,128)S(1)}, f32[128,128]{1,0:T(8,128)S(1)}, u32[]{:S(2)}, u32[]{:S(2)}) collective-permute-start(f32[128,128]{1,0:T(8,128)S(1)} %get-tuple-element.14), channel_id=1, source_target_pairs={{0,32},{32,0},{64,96},{96,64},{1,33},{33,1},{65,97},{97,65},{2,34}... | collective-permute-start | bytes 196616 | tf_op jit(solution)/shard_map/ppermute | solution.py:286
  21.9 5.7 %collective-permute-start.2 = (f32[32,128]{1,0:T(8,128)S(1)}, f32[32,128]{1,0:T(8,128)S(1)}, u32[]{:S(2)}, u32[]{:S(2)}) collective-permute-start(f32[32,128]{1,0:T(8,128)S(1)} %get-tuple-element.15), channel_id=1, source_target_pairs={{0,1},{1,0},{2,3},{3,2},{4,5},{5,4},{6,7},{7,6},{8,9},{9,8},{10,11... | collective-permute-start | bytes 49160 | tf_op jit(solution)/shard_map/ppermute | solution.py:289
  25.8 4.9 %collective-permute-start.4 = (f32[32,128]{1,0:T(8,128)S(1)}, f32[32,128]{1,0:T(8,128)S(1)}, u32[]{:S(2)}, u32[]{:S(2)}) collective-permute-start(f32[32,128]{1,0:T(8,128)S(1)} %get-tuple-element.16), channel_id=1, source_target_pairs={{0,65},{1,64},{2,67},{3,66},{4,69},{5,68},{6,71},{7,70},{8,73},{9,... | collective-permute-start | bytes 49160 | tf_op jit(solution)/shard_map/ppermute | solution.py:289
  26.6 4.2 %collective-permute-start.3 = (f32[32,128]{1,0:T(8,128)S(1)}, f32[32,128]{1,0:T(8,128)S(1)}, u32[]{:S(2)}, u32[]{:S(2)}) collective-permute-start(f32[32,128]{1,0:T(8,128)S(1)} %get-tuple-element.17), channel_id=1, source_target_pairs={{0,64},{1,65},{2,66},{3,67},{4,68},{5,69},{6,70},{7,71},{8,72},{9,... | collective-permute-start | bytes 49160 | tf_op jit(solution)/shard_map/ppermute | solution.py:289

commit v7 on v3

--- a/solution.py
+++ b/solution.py
@@ -45,10 +45,12 @@
     ]
     for copy in copies:
         copy.start()
-    for copy in copies:
-        copy.wait()
+    copies[0].wait()
     rows = weight_ref.shape[1]
     flags = flag_ref[...].astype(jnp.float32)
+    spot = jnp.where(flags > 0.0, lane_prefix(flags), -1.0).astype(jnp.int32)
+    for copy in copies[1:]:
+        copy.wait()
     weights = weight_ref[...]
     data_ref[0:2, :] = vis_ref[:, 0, :] * weights
     data_ref[2:4, :] = vis_ref[:, 1, :] * weights
@@ -60,7 +62,6 @@
     middle = rest.astype(jnp.bfloat16).astype(jnp.float32)
     low = rest - middle
     pieces = jnp.concatenate([high, middle, low], axis=0).astype(jnp.bfloat16)
-    spot = jnp.where(flags > 0.0, lane_prefix(flags), -1.0).astype(jnp.int32)
     target = lax.broadcasted_iota(jnp.int32, (KEEP, rows), 0)
     packed = []
     for block in range(2):
@@ -198,15 +199,13 @@
     buffers = (scratch[0:4], scratch[4:8])
     source = (which, centre_ref, data_ref, gain_ref)
     steps = data_ref.shape[0] // 64
-    prepare(*source, 0, 0, buffers[0])
-
-    def advance(step, sums):
-        prepare(*source, step, 1, buffers[1])
-        sums = accumulate(buffers[0], sums)
-        prepare(*source, (step + 1) & (steps - 1), 0, buffers[0])
-        return accumulate(buffers[1], sums)
-
-    return lax.fori_loop(0, steps, advance, sums)
+    groups = [(step, half) for step in range(steps) for half in range(2)]
+    prepare(*source, *groups[0], buffers[0])
+    for index in range(len(groups)):
+        if index + 1 < len(groups):
+            prepare(*source, *groups[index + 1], buffers[(index + 1) % 2])
+        sums = accumulate(buffers[index % 2], sums)
+    return sums
 
 
 def first_kernel(centre_ref, gain_ref, data_ref, even_ref, odd_ref, *scratch):

time: 31.3 us -> 30.8 us (0.984)
  Pallas kernels: 5.79 us -> 5.01 us
  waiting for transfers between devices: 4.1 us -> 4.47 us
    ppermute x1, waiting for transfers between devices: 0.74 us -> 1.11 us  [body(): far = lax.ppermute(near, 'facet', [(i, i ^ 1) for i in range(2 * plane)])]
    pallas_call x1, Pallas kernels: 2.2 us -> 1.84 us  [body(): pl.pallas_call(first_kernel, out_shape=(image, image), in_specs=[VMEM] *...]
    pallas_call x1, Pallas kernels: 2.34 us -> 1.98 us  [body(): pl.pallas_call(functools.partial(last_kernel, 2.0 / math.sqrt(total)), ou...]
  transfers between devices with their start and end apart: 3 -> 3, of which waited for: 3 -> 3; matrix products, arithmetic and copies ran while one was open for 0% -> 0% of each run, Pallas kernels for 7% -> 6%
where the time goes in v7:
time: 30.8 us; the launch traced here: 30.7 us
  blocking collectives  14.9 us (48%)
  starting transfers between devices  5.61 us (18%)
  Pallas kernels  5.01 us (16%)
  waiting for transfers between devices  4.47 us (15%)
  other arithmetic  0.61 us (2%)
    all_to_all x1, blocking collectives, body(): near = lax.all_to_all(packed, 'facet', 0, 0, axis_index_groups=groups)  14.9 us
    ppermute x1, starting transfers between devices, body(): far = lax.ppermute(near, 'facet', [(i, i ^ 1) for i in range(2 * plane)])  3.88 us
    ppermute x1, waiting for transfers between devices, body(): lax.ppermute(half[32:], 'freq', [(i, i ^ 2) for i in range(4)])  2.17 us
    pallas_call x1, Pallas kernels, body(): pl.pallas_call(functools.partial(last_kernel, 2.0 / math.sqrt(total)), ou...  1.98 us
    pallas_call x1, Pallas kernels, body(): pl.pallas_call(first_kernel, out_shape=(image, image), in_specs=[VMEM] *...  1.84 us
    ppermute x1, starting transfers between devices, body(): lax.ppermute(half[32:], 'freq', [(i, i ^ 2) for i in range(4)])  1.65 us
    pallas_call x1, Pallas kernels, body(): pl.pallas_call(pack_kernel, out_shape=(jax.ShapeDtypeStruct((plane, 16, L...  1.19 us
    ppermute x1, waiting for transfers between devices, body(): half = keep + lax.ppermute(send, 'freq', [(i, i ^ 1) for i in range(4)])  1.19 us
  transfers between devices with their start and end apart: 3, of which 3 were waited for; matrix products, arithmetic and copies ran while one was open for 0% of the time, Pallas kernels for 6%

profile of v7, /device:TPU:0, one launch (start us, length us, event | category | flops | bytes accessed | tf_op | source)
XLA Modules:
  0.0 30.7 jit_solution(2165056140545366819)
XLA Ops:
  0.0 1.2 %shard_map.73 = (f32[16,16,128]{2,1,0:T(8,128)S(1)}, f32[64,128]{1,0:T(8,128)S(1)}, s32[16,128]{1,0:T(8,128)S(1)}) custom-call(f32[2,2,512]{2,1,0:T(2,128)} %vis_in.1, f32[2,512]{1,0:T(2,128)} %weight_in.1, s32[2,2,512]{2,1,0:T(2,128)} %uv_in.1, s32[2,512]{1,0:T(2,128)} %flag_in.1, s32[1,64]{1,0:T(1,128)} %bitcast.6, f32[1,64]{1,0:T(1,128)} %beam_in.1, ...), custom_call_target="tpu_custom_call" | custom-call | tf_op jit(solution)/shard_map/pallas_call | solution.py:258
  1.2 14.9 %all_to_all.5 = f32[16,16,128]{2,1,0:T(8,128)S(1)} all-to-all(f32[16,16,128]{2,1,0:T(8,128)S(1)} %get-tuple-element.14), channel_id=1, replica_groups={{0,2,4,6,8,10,12,14,16,18,20,22,24,26,28,30},{1,3,5,7,9,11,13,15,17,19,..., dimensions={0} | all-to-all | bytes 262144 | tf_op jit(solution)/shard_map/all_to_all | solution.py:275
  16.1 3.9 %collective-permute-start = (f32[256,128]{1,0:T(8,128)S(1)}, f32[256,128]{1,0:T(8,128)S(1)}, u32[]{:S(2)}, u32[]{:S(2)}) collective-permute-start(f32[256,128]{1,0:T(8,128)S(1)} %bitcast.4), channel_id=1, source_target_pairs={{0,1},{1,0},{2,3},{3,2},{4,5},{5,4},{6,7},{7,6},{8,9},{9,8},{10,11... | collective-permute-start | bytes 393224 | tf_op jit(solution)/shard_map/ppermute | solution.py:277
  20.0 1.8 %shard_map.74 = (f32[64,128]{1,0:T(8,128)S(1)}, f32[64,128]{1,0:T(8,128)S(1)}) custom-call(s32[16,128]{1,0:T(8,128)S(1)} %get-tuple-element.12.centre_ref, f32[64,128]{1,0:T(8,128)S(1)} %get-tuple-element.13.gain_ref, f32[256,128]{1,0:T(8,128)S(1)} %bitcast.5), custom_call_target="tpu_custom_call" | custom-call | flops 268435456 | bytes 262144 | tf_op jit(solution)/shard_map/pallas_call | solution.py:289
  21.9 1.1 %collective-permute-done.data_ref = f32[256,128]{1,0:T(8,128)S(1)} collective-permute-done((f32[256,128]{1,0:T(8,128)S(1)}, f32[256,128]{1,0:T(8,128)S(1)}, u32[]{:S(2)}, u32[]{:S(2)}) %collective-permute-start) | collective-permute-done | bytes 131104 | tf_op jit(solution)/shard_map/ppermute | solution.py:277
  23.0 2.0 %shard_map.75 = (f32[64,128]{1,0:T(8,128)S(1)}, f32[64,128]{1,0:T(8,128)S(1)}) custom-call(s32[16,128]{1,0:T(8,128)S(1)} %get-tuple-element.12.centre_ref, f32[64,128]{1,0:T(8,128)S(1)} %get-tuple-element.13.gain_ref, f32[256,128]{1,0:T(8,128)S(1)} %collective-permute-done.data_ref, f32[64,128]{1,0:T(8,128)S(1)} %get-tuple-element.15.even_ref, ...), custom_call_target="tpu_custom_call" | custom-call | flops 268435456 | bytes 262144 | tf_op jit(solution)/shard_map/pallas_call | solution.py:298
  24.9 0.1 collective-permute-start.1
  25.0 1.2 %collective-permute-done.1 = f32[64,128]{1,0:T(8,128)S(1)} collective-permute-done((f32[64,128]{1,0:T(8,128)S(1)}, f32[64,128]{1,0:T(8,128)S(1)}, u32[]{:S(2)}, u32[]{:S(2)}) %collective-permute-start.1) | collective-permute-done | bytes 32800 | tf_op jit(solution)/shard_map/ppermute | solution.py:307
  26.2 1.6 %collective-permute-start.2 = (f32[32,128]{1,0:T(8,128)S(1)}, f32[32,128]{1,0:T(8,128)S(1)}, u32[]{:S(2)}, u32[]{:S(2)}) collective-permute-start(f32[32,128]{1,0:T(8,128)S(1)} %slice.9), channel_id=1, source_target_pairs={{0,64},{32,96},{64,0},{96,32},{1,65},{33,97},{65,1},{97,33},{2,66}... | collective-permute-start | bytes 49160 | tf_op jit(solution)/shard_map/ppermute | solution.py:308
  27.9 2.2 %collective-permute-done.2 = f32[32,128]{1,0:T(8,128)S(1)} collective-permute-done((f32[32,128]{1,0:T(8,128)S(1)}, f32[32,128]{1,0:T(8,128)S(1)}, u32[]{:S(2)}, u32[]{:S(2)}) %collective-permute-start.2) | collective-permute-done | bytes 16416 | tf_op jit(solution)/shard_map/ppermute | solution.py:308
  30.1 0.6 %fusion = f32[1,32,128]{2,1,0:T(8,128)} fusion(f32[32,128]{1,0:T(8,128)S(1)} %collective-permute-done.2, f32[64,128]{1,0:T(8,128)S(1)} %add.6), kind=kLoop, calls=%fused_computation.1 | loop fusion | flops 4096 | bytes 49152 | tf_op jit(solution)/shard_map/broadcast_in_dim | solution.py:308
  (2 shorter events, 0.0 us)
Async XLA Ops:
  16.1 6.8 %collective-permute-start = (f32[256,128]{1,0:T(8,128)S(1)}, f32[256,128]{1,0:T(8,128)S(1)}, u32[]{:S(2)}, u32[]{:S(2)}) collective-permute-start(f32[256,128]{1,0:T(8,128)S(1)} %bitcast.4), channel_id=1, source_target_pairs={{0,1},{1,0},{2,3},{3,2},{4,5},{5,4},{6,7},{7,6},{8,9},{9,8},{10,11... | collective-permute-start | bytes 393224 | tf_op jit(solution)/shard_map/ppermute | solution.py:277
  24.9 1.3 %collective-permute-start.1 = (f32[64,128]{1,0:T(8,128)S(1)}, f32[64,128]{1,0:T(8,128)S(1)}, u32[]{:S(2)}, u32[]{:S(2)}) collective-permute-start(f32[64,128]{1,0:T(8,128)S(1)} %get-tuple-element.18), channel_id=1, source_target_pairs={{0,32},{32,0},{64,96},{96,64},{1,33},{33,1},{65,97},{97,65},{2,34}... | collective-permute-start | bytes 98312 | tf_op jit(solution)/shard_map/ppermute | solution.py:307
  26.2 3.8 %collective-permute-start.2 = (f32[32,128]{1,0:T(8,128)S(1)}, f32[32,128]{1,0:T(8,128)S(1)}, u32[]{:S(2)}, u32[]{:S(2)}) collective-permute-start(f32[32,128]{1,0:T(8,128)S(1)} %slice.9), channel_id=1, source_target_pairs={{0,64},{32,96},{64,0},{96,32},{1,65},{33,97},{65,1},{97,33},{2,66}... | collective-permute-start | bytes 49160 | tf_op jit(solution)/shard_map/ppermute | solution.py:308

commit v8 on v7

--- a/solution.py
+++ b/solution.py
@@ -196,15 +196,15 @@
 
 
 def sum_blocks(which, centre_ref, gain_ref, data_ref, scratch, sums):
-    buffers = (scratch[0:4], scratch[4:8])
+    buffers = [scratch[4 * k : 4 * k + 4] for k in range(8)]
     source = (which, centre_ref, data_ref, gain_ref)
     steps = data_ref.shape[0] // 64
     groups = [(step, half) for step in range(steps) for half in range(2)]
     prepare(*source, *groups[0], buffers[0])
     for index in range(len(groups)):
         if index + 1 < len(groups):
-            prepare(*source, *groups[index + 1], buffers[(index + 1) % 2])
-        sums = accumulate(buffers[index % 2], sums)
+            prepare(*source, *groups[index + 1], buffers[(index + 1) % 8])
+        sums = accumulate(buffers[index % 8], sums)
     return sums
 
 
@@ -282,7 +282,7 @@
         pltpu.VMEM((16, 8, LANES), jnp.float32),
         pltpu.VMEM((8, 8, LANES), jnp.float32),
     ]
-    scratch = buffers * 2
+    scratch = buffers * 8
     cost = pl.CostEstimate(
         flops=2 * 2 * HALF * P_SIZE * 2 * plane * KEEP, bytes_accessed=1 << 18, transcendentals=0
     )

time: 30.8 us -> 30.7 us (level)
  Pallas kernels: 5.01 us -> 4.67 us
  transfers between devices with their start and end apart: 3 -> 3, of which waited for: 3 -> 3; matrix products, arithmetic and copies ran while one was open for 0% -> 0% of each run, Pallas kernels for 6% -> 5%
where the time goes in v8:
time: 30.7 us; the launch traced here: 30.5 us
  blocking collectives  14.9 us (49%)
  starting transfers between devices  5.61 us (18%)
  Pallas kernels  4.67 us (15%)
  waiting for transfers between devices  4.65 us (15%)
  other arithmetic  0.61 us (2%)
    all_to_all x1, blocking collectives, body(): near = lax.all_to_all(packed, 'facet', 0, 0, axis_index_groups=groups)  14.9 us
    ppermute x1, starting transfers between devices, body(): far = lax.ppermute(near, 'facet', [(i, i ^ 1) for i in range(2 * plane)])  3.88 us
    ppermute x1, waiting for transfers between devices, body(): lax.ppermute(half[32:], 'freq', [(i, i ^ 2) for i in range(4)])  2.17 us
    pallas_call x1, Pallas kernels, body(): pl.pallas_call(functools.partial(last_kernel, 2.0 / math.sqrt(total)), ou...  1.82 us
    pallas_call x1, Pallas kernels, body(): pl.pallas_call(first_kernel, out_shape=(image, image), in_specs=[VMEM] *...  1.66 us
    ppermute x1, starting transfers between devices, body(): lax.ppermute(half[32:], 'freq', [(i, i ^ 2) for i in range(4)])  1.65 us
    ppermute x1, waiting for transfers between devices, body(): far = lax.ppermute(near, 'facet', [(i, i ^ 1) for i in range(2 * plane)])  1.29 us
    pallas_call x1, Pallas kernels, body(): pl.pallas_call(pack_kernel, out_shape=(jax.ShapeDtypeStruct((plane, 16, L...  1.19 us
  transfers between devices with their start and end apart: 3, of which 3 were waited for; matrix products, arithmetic and copies ran while one was open for 0% of the time, Pallas kernels for 5%

profile of v8, /device:TPU:0, one launch (start us, length us, event | category | flops | bytes accessed | tf_op | source)
XLA Modules:
  0.0 30.5 jit_solution(8837699555640895486)
XLA Ops:
  0.0 1.2 %shard_map.73 = (f32[16,16,128]{2,1,0:T(8,128)S(1)}, f32[64,128]{1,0:T(8,128)S(1)}, s32[16,128]{1,0:T(8,128)S(1)}) custom-call(f32[2,2,512]{2,1,0:T(2,128)} %vis_in.1, f32[2,512]{1,0:T(2,128)} %weight_in.1, s32[2,2,512]{2,1,0:T(2,128)} %uv_in.1, s32[2,512]{1,0:T(2,128)} %flag_in.1, s32[1,64]{1,0:T(1,128)} %bitcast.6, f32[1,64]{1,0:T(1,128)} %beam_in.1, ...), custom_call_target="tpu_custom_call" | custom-call | tf_op jit(solution)/shard_map/pallas_call | solution.py:258
  1.2 14.9 %all_to_all.5 = f32[16,16,128]{2,1,0:T(8,128)S(1)} all-to-all(f32[16,16,128]{2,1,0:T(8,128)S(1)} %get-tuple-element.14), channel_id=1, replica_groups={{0,2,4,6,8,10,12,14,16,18,20,22,24,26,28,30},{1,3,5,7,9,11,13,15,17,19,..., dimensions={0} | all-to-all | bytes 262144 | tf_op jit(solution)/shard_map/all_to_all | solution.py:275
  16.1 3.9 %collective-permute-start = (f32[256,128]{1,0:T(8,128)S(1)}, f32[256,128]{1,0:T(8,128)S(1)}, u32[]{:S(2)}, u32[]{:S(2)}) collective-permute-start(f32[256,128]{1,0:T(8,128)S(1)} %bitcast.4), channel_id=1, source_target_pairs={{0,1},{1,0},{2,3},{3,2},{4,5},{5,4},{6,7},{7,6},{8,9},{9,8},{10,11... | collective-permute-start | bytes 393224 | tf_op jit(solution)/shard_map/ppermute | solution.py:277
  20.0 1.7 %shard_map.74 = (f32[64,128]{1,0:T(8,128)S(1)}, f32[64,128]{1,0:T(8,128)S(1)}) custom-call(s32[16,128]{1,0:T(8,128)S(1)} %get-tuple-element.12.centre_ref, f32[64,128]{1,0:T(8,128)S(1)} %get-tuple-element.13.gain_ref, f32[256,128]{1,0:T(8,128)S(1)} %bitcast.5), custom_call_target="tpu_custom_call" | custom-call | flops 268435456 | bytes 262144 | tf_op jit(solution)/shard_map/pallas_call | solution.py:289
  21.7 1.3 %collective-permute-done.data_ref = f32[256,128]{1,0:T(8,128)S(1)} collective-permute-done((f32[256,128]{1,0:T(8,128)S(1)}, f32[256,128]{1,0:T(8,128)S(1)}, u32[]{:S(2)}, u32[]{:S(2)}) %collective-permute-start) | collective-permute-done | bytes 131104 | tf_op jit(solution)/shard_map/ppermute | solution.py:277
  23.0 1.8 %shard_map.75 = (f32[64,128]{1,0:T(8,128)S(1)}, f32[64,128]{1,0:T(8,128)S(1)}) custom-call(s32[16,128]{1,0:T(8,128)S(1)} %get-tuple-element.12.centre_ref, f32[64,128]{1,0:T(8,128)S(1)} %get-tuple-element.13.gain_ref, f32[256,128]{1,0:T(8,128)S(1)} %collective-permute-done.data_ref, f32[64,128]{1,0:T(8,128)S(1)} %get-tuple-element.15.even_ref, ...), custom_call_target="tpu_custom_call" | custom-call | flops 268435456 | bytes 262144 | tf_op jit(solution)/shard_map/pallas_call | solution.py:298
  24.8 0.1 collective-permute-start.1
  24.9 1.2 %collective-permute-done.1 = f32[64,128]{1,0:T(8,128)S(1)} collective-permute-done((f32[64,128]{1,0:T(8,128)S(1)}, f32[64,128]{1,0:T(8,128)S(1)}, u32[]{:S(2)}, u32[]{:S(2)}) %collective-permute-start.1) | collective-permute-done | bytes 32800 | tf_op jit(solution)/shard_map/ppermute | solution.py:307
  26.1 1.6 %collective-permute-start.2 = (f32[32,128]{1,0:T(8,128)S(1)}, f32[32,128]{1,0:T(8,128)S(1)}, u32[]{:S(2)}, u32[]{:S(2)}) collective-permute-start(f32[32,128]{1,0:T(8,128)S(1)} %slice.9), channel_id=1, source_target_pairs={{0,64},{32,96},{64,0},{96,32},{1,65},{33,97},{65,1},{97,33},{2,66}... | collective-permute-start | bytes 49160 | tf_op jit(solution)/shard_map/ppermute | solution.py:308
  27.7 2.2 %collective-permute-done.2 = f32[32,128]{1,0:T(8,128)S(1)} collective-permute-done((f32[32,128]{1,0:T(8,128)S(1)}, f32[32,128]{1,0:T(8,128)S(1)}, u32[]{:S(2)}, u32[]{:S(2)}) %collective-permute-start.2) | collective-permute-done | bytes 16416 | tf_op jit(solution)/shard_map/ppermute | solution.py:308
  29.9 0.6 %fusion = f32[1,32,128]{2,1,0:T(8,128)} fusion(f32[32,128]{1,0:T(8,128)S(1)} %collective-permute-done.2, f32[64,128]{1,0:T(8,128)S(1)} %add.6), kind=kLoop, calls=%fused_computation.1 | loop fusion | flops 4096 | bytes 49152 | tf_op jit(solution)/shard_map/broadcast_in_dim | solution.py:308
  (2 shorter events, 0.0 us)
Async XLA Ops:
  16.1 6.8 %collective-permute-start = (f32[256,128]{1,0:T(8,128)S(1)}, f32[256,128]{1,0:T(8,128)S(1)}, u32[]{:S(2)}, u32[]{:S(2)}) collective-permute-start(f32[256,128]{1,0:T(8,128)S(1)} %bitcast.4), channel_id=1, source_target_pairs={{0,1},{1,0},{2,3},{3,2},{4,5},{5,4},{6,7},{7,6},{8,9},{9,8},{10,11... | collective-permute-start | bytes 393224 | tf_op jit(solution)/shard_map/ppermute | solution.py:277
  24.8 1.3 %collective-permute-start.1 = (f32[64,128]{1,0:T(8,128)S(1)}, f32[64,128]{1,0:T(8,128)S(1)}, u32[]{:S(2)}, u32[]{:S(2)}) collective-permute-start(f32[64,128]{1,0:T(8,128)S(1)} %get-tuple-element.18), channel_id=1, source_target_pairs={{0,32},{32,0},{64,96},{96,64},{1,33},{33,1},{65,97},{97,65},{2,34}... | collective-permute-start | bytes 98312 | tf_op jit(solution)/shard_map/ppermute | solution.py:307
  26.1 3.8 %collective-permute-start.2 = (f32[32,128]{1,0:T(8,128)S(1)}, f32[32,128]{1,0:T(8,128)S(1)}, u32[]{:S(2)}, u32[]{:S(2)}) collective-permute-start(f32[32,128]{1,0:T(8,128)S(1)} %slice.9), channel_id=1, source_target_pairs={{0,64},{32,96},{64,0},{96,32},{1,65},{33,97},{65,1},{97,33},{2,66}... | collective-permute-start | bytes 49160 | tf_op jit(solution)/shard_map/ppermute | solution.py:308

commit v9 on v8

--- a/solution.py
+++ b/solution.py
@@ -30,16 +30,15 @@
 
 
 def pack_kernel(
-    vis_in, weight_in, uv_in, flag_in, plan_in, beam_in, facet_in,
-    out_ref, gain_ref, centre_ref,
-    vis_ref, weight_ref, uv_ref, flag_ref, plan_ref, beam_ref, facet_ref, data_ref, arrived,
+    vis_in, weight_in, uv_in, flag_in,
+    out_ref,
+    vis_ref, weight_ref, uv_ref, flag_ref, data_ref, arrived,
 ):
     copies = [
         pltpu.make_async_copy(source, target, arrived.at[index])
         for index, (source, target) in enumerate(
             (
                 (flag_in, flag_ref), (vis_in, vis_ref), (weight_in, weight_ref), (uv_in, uv_ref),
-                (plan_in, plan_ref), (beam_in, beam_ref), (facet_in, facet_ref),
             )
         )
     ]
@@ -76,18 +75,6 @@
     for peer in range(plane):
         out_ref[peer, 0:8, :] = result[:, :LANES]
         out_ref[peer, 8:16, :] = result[:, LANES:]
-    side = lax.axis_index("facet") & 1
-    shape = (plane, plan_ref.shape[1])
-    for which in range(2):
-        for member in range(2):
-            block = 4 * lax.broadcasted_iota(jnp.int32, shape, 0) + 2 * (side ^ which) + member
-            matches = plan_ref[...] == block
-            gain = jnp.sum(jnp.where(matches, beam_ref[...], 0.0), axis=1, keepdims=True)
-            first = (2 * which + member) * plane
-            gain_ref[first : first + plane, :] = jnp.broadcast_to(gain, (plane, LANES))
-    for axis in range(2):
-        centre = 2 * (facet_ref[0:1, axis : axis + 1] * P_SIZE - IMG // 2) + (P_SIZE - 1)
-        centre_ref[8 * axis : 8 * axis + 8, :] = jnp.broadcast_to(centre, (8, LANES))
 
 
 def doubled(sine, cosine):
@@ -208,7 +195,33 @@
     return sums
 
 
-def first_kernel(centre_ref, gain_ref, data_ref, even_ref, odd_ref, *scratch):
+def first_kernel(
+    plan_in, beam_in, facet_in, data_ref, even_ref, odd_ref, gain_ref, centre_ref,
+    plan_ref, beam_ref, facet_ref, arrived, *scratch,
+):
+    copies = [
+        pltpu.make_async_copy(source, target, arrived.at[index])
+        for index, (source, target) in enumerate(
+            ((plan_in, plan_ref), (beam_in, beam_ref), (facet_in, facet_ref))
+        )
+    ]
+    for copy in copies:
+        copy.start()
+    for copy in copies:
+        copy.wait()
+    plane = gain_ref.shape[0] // 4
+    side = lax.axis_index("facet") & 1
+    shape = (plane, plan_ref.shape[1])
+    for which in range(2):
+        for member in range(2):
+            block = 4 * lax.broadcasted_iota(jnp.int32, shape, 0) + 2 * (side ^ which) + member
+            matches = plan_ref[...] == block
+            gain = jnp.sum(jnp.where(matches, beam_ref[...], 0.0), axis=1, keepdims=True)
+            first = (2 * which + member) * plane
+            gain_ref[first : first + plane, :] = jnp.broadcast_to(gain, (plane, LANES))
+    for axis in range(2):
+        centre = 2 * (facet_ref[0:1, axis : axis + 1] * P_SIZE - IMG // 2) + (P_SIZE - 1)
+        centre_ref[8 * axis : 8 * axis + 8, :] = jnp.broadcast_to(centre, (8, LANES))
     zero = jnp.zeros((HALF, P_SIZE), jnp.float32)
     even, odd = sum_blocks(0, centre_ref, gain_ref, data_ref, scratch, (zero, zero))
     even_ref[...] = even
@@ -254,23 +267,23 @@
 
 
 def body(total, plane, visibilities, weights, uv_cells, flags, plan, beam, facets):
-    arguments = (visibilities, weights, uv_cells, flags, plan[None], beam, facets)
-    packed, gains, centre = pl.pallas_call(
+    def in_hbm(*arrays):
+        return [pltpu.with_memory_space_constraint(each, pltpu.HBM) for each in arrays]
+
+    arguments = (visibilities, weights, uv_cells, flags)
+    packed = pl.pallas_call(
         pack_kernel,
-        out_shape=(
-            jax.ShapeDtypeStruct((plane, 16, LANES), jnp.float32),
-            jax.ShapeDtypeStruct((4 * plane, LANES), jnp.float32),
-            jax.ShapeDtypeStruct((16, LANES), jnp.int32),
-        ),
-        in_specs=[pl.BlockSpec(memory_space=pltpu.HBM)] * 7,
-        out_specs=(VMEM, VMEM, VMEM),
+        out_shape=jax.ShapeDtypeStruct((plane, 16, LANES), jnp.float32),
+        in_specs=[pl.BlockSpec(memory_space=pltpu.HBM)] * 4,
+        out_specs=VMEM,
         scratch_shapes=[pltpu.VMEM(each.shape, each.dtype) for each in arguments]
         + [
             pltpu.VMEM((8, weights.shape[1]), jnp.float32),
             pltpu.SemaphoreType.DMA((len(arguments),)),
         ],
         compiler_params=SMALL,
-    )(*(pltpu.with_memory_space_constraint(each, pltpu.HBM) for each in arguments))
+    )(*in_hbm(*arguments))
+    notes = (plan[None], beam, facets)
     groups = [list(range(side, 2 * plane, 2)) for side in range(2)]
     near = lax.all_to_all(packed, "facet", 0, 0, axis_index_groups=groups)
     near = near.reshape(plane * 16, LANES)
@@ -286,15 +299,22 @@
     cost = pl.CostEstimate(
         flops=2 * 2 * HALF * P_SIZE * 2 * plane * KEEP, bytes_accessed=1 << 18, transcendentals=0
     )
-    even, odd = pl.pallas_call(
+    even, odd, gains, centre = pl.pallas_call(
         first_kernel,
-        out_shape=(image, image),
-        in_specs=[VMEM] * 3,
-        out_specs=(VMEM, VMEM),
-        scratch_shapes=scratch,
+        out_shape=(
+            image,
+            image,
+            jax.ShapeDtypeStruct((4 * plane, LANES), jnp.float32),
+            jax.ShapeDtypeStruct((16, LANES), jnp.int32),
+        ),
+        in_specs=[pl.BlockSpec(memory_space=pltpu.HBM)] * 3 + [VMEM],
+        out_specs=(VMEM,) * 4,
+        scratch_shapes=[pltpu.VMEM(each.shape, each.dtype) for each in notes]
+        + [pltpu.SemaphoreType.DMA((3,))]
+        + scratch,
         compiler_params=SMALL,
         cost_estimate=cost,
-    )(centre, gains, near)
+    )(*in_hbm(*notes), near)
     keep, send = pl.pallas_call(
         functools.partial(last_kernel, 2.0 / math.sqrt(total)),
         out_shape=(image, image),

time: 30.7 us -> 30.7 us (level)
  waiting for transfers between devices: 4.65 us -> 3.81 us
  Pallas kernels: 4.67 us -> 5.47 us
    ppermute x1, waiting for transfers between devices: 1.29 us -> 0.45 us  [body(): far = lax.ppermute(near, 'facet', [(i, i ^ 1) for i in range(2 * plane)])]
    pallas_call x2, Pallas kernels: 2.85 us -> 3.65 us  [the longest x1 2.49 us: body(): pl.pallas_call(first_kernel, out_shape=(image, image, jax.ShapeDtypeStruc...]
  transfers between devices with their start and end apart: 3 -> 3, of which waited for: 3 -> 3; matrix products, arithmetic and copies ran while one was open for 0% -> 0% of each run, Pallas kernels for 5% -> 8%
where the time goes in v9:
time: 30.7 us; the launch traced here: 30.5 us
  blocking collectives  14.9 us (49%)
  starting transfers between devices  5.61 us (18%)
  Pallas kernels  5.47 us (18%)
  waiting for transfers between devices  3.81 us (12%)
  other arithmetic  0.61 us (2%)
    all_to_all x1, blocking collectives, body(): near = lax.all_to_all(packed, 'facet', 0, 0, axis_index_groups=groups)  14.9 us
    ppermute x1, starting transfers between devices, body(): far = lax.ppermute(near, 'facet', [(i, i ^ 1) for i in range(2 * plane)])  3.88 us
    pallas_call x1, Pallas kernels, body(): pl.pallas_call(first_kernel, out_shape=(image, image, jax.ShapeDtypeStruc...  2.49 us
    ppermute x1, waiting for transfers between devices, body(): lax.ppermute(half[32:], 'freq', [(i, i ^ 2) for i in range(4)])  2.17 us
    pallas_call x1, Pallas kernels, body(): pl.pallas_call(functools.partial(last_kernel, 2.0 / math.sqrt(total)), ou...  1.81 us
    ppermute x1, starting transfers between devices, body(): lax.ppermute(half[32:], 'freq', [(i, i ^ 2) for i in range(4)])  1.65 us
    ppermute x1, waiting for transfers between devices, body(): half = keep + lax.ppermute(send, 'freq', [(i, i ^ 1) for i in range(4)])  1.19 us
    pallas_call x1, Pallas kernels, body(): pl.pallas_call(pack_kernel, out_shape=jax.ShapeDtypeStruct((plane, 16, LA...  1.16 us
  transfers between devices with their start and end apart: 3, of which 3 were waited for; matrix products, arithmetic and copies ran while one was open for 0% of the time, Pallas kernels for 8%

profile of v9, /device:TPU:0, one launch (start us, length us, event | category | flops | bytes accessed | tf_op | source)
XLA Modules:
  0.0 30.5 jit_solution(11003295330997362983)
XLA Ops:
  0.0 1.2 %shard_map.73 = f32[16,16,128]{2,1,0:T(8,128)S(1)} custom-call(f32[2,2,512]{2,1,0:T(2,128)} %vis_in.1, f32[2,512]{1,0:T(2,128)} %weight_in.1, s32[2,2,512]{2,1,0:T(2,128)} %uv_in.1, s32[2,512]{1,0:T(2,128)} %flag_in.1), custom_call_target="tpu_custom_call" | custom-call | tf_op jit(solution)/shard_map/pallas_call | solution.py:274
  1.2 14.9 %all_to_all.5 = f32[16,16,128]{2,1,0:T(8,128)S(1)} all-to-all(f32[16,16,128]{2,1,0:T(8,128)S(1)} %shard_map.73), channel_id=1, replica_groups={{0,2,4,6,8,10,12,14,16,18,20,22,24,26,28,30},{1,3,5,7,9,11,13,15,17,19,..., dimensions={0} | all-to-all | bytes 262144 | tf_op jit(solution)/shard_map/all_to_all | solution.py:288
  16.1 3.9 %collective-permute-start = (f32[256,128]{1,0:T(8,128)S(1)}, f32[256,128]{1,0:T(8,128)S(1)}, u32[]{:S(2)}, u32[]{:S(2)}) collective-permute-start(f32[256,128]{1,0:T(8,128)S(1)} %bitcast.4), channel_id=1, source_target_pairs={{0,1},{1,0},{2,3},{3,2},{4,5},{5,4},{6,7},{7,6},{8,9},{9,8},{10,11... | collective-permute-start | bytes 393224 | tf_op jit(solution)/shard_map/ppermute | solution.py:290
  20.0 2.5 %shard_map.74 = (f32[64,128]{1,0:T(8,128)S(1)}, f32[64,128]{1,0:T(8,128)S(1)}, f32[64,128]{1,0:T(8,128)S(1)}, s32[16,128]{1,0:T(8,128)S(1)}) custom-call(s32[1,64]{1,0:T(1,128)} %bitcast.6, f32[1,64]{1,0:T(1,128)} %beam_in.1, s32[1,2]{1,0:T(1,128)} %facet_in.1, f32[256,128]{1,0:T(8,128)S(1)} %bitcast.5), custom_call_target="tpu_custom_call" | custom-call | flops 268435456 | bytes 262144 | tf_op jit(solution)/shard_map/pallas_call | solution.py:302
  22.5 0.4 %collective-permute-done.data_ref = f32[256,128]{1,0:T(8,128)S(1)} collective-permute-done((f32[256,128]{1,0:T(8,128)S(1)}, f32[256,128]{1,0:T(8,128)S(1)}, u32[]{:S(2)}, u32[]{:S(2)}) %collective-permute-start) | collective-permute-done | bytes 131104 | tf_op jit(solution)/shard_map/ppermute | solution.py:290
  22.9 1.8 %shard_map.75 = (f32[64,128]{1,0:T(8,128)S(1)}, f32[64,128]{1,0:T(8,128)S(1)}) custom-call(s32[16,128]{1,0:T(8,128)S(1)} %get-tuple-element.11.centre_ref, f32[64,128]{1,0:T(8,128)S(1)} %get-tuple-element.12.gain_ref, f32[256,128]{1,0:T(8,128)S(1)} %collective-permute-done.data_ref, f32[64,128]{1,0:T(8,128)S(1)} %get-tuple-element.13.even_ref, ...), custom_call_target="tpu_custom_call" | custom-call | flops 268435456 | bytes 262144 | tf_op jit(solution)/shard_map/pallas_call | solution.py:318
  24.7 0.1 collective-permute-start.1
  24.8 1.2 %collective-permute-done.1 = f32[64,128]{1,0:T(8,128)S(1)} collective-permute-done((f32[64,128]{1,0:T(8,128)S(1)}, f32[64,128]{1,0:T(8,128)S(1)}, u32[]{:S(2)}, u32[]{:S(2)}) %collective-permute-start.1) | collective-permute-done | bytes 32800 | tf_op jit(solution)/shard_map/ppermute | solution.py:327
  26.0 1.6 %collective-permute-start.2 = (f32[32,128]{1,0:T(8,128)S(1)}, f32[32,128]{1,0:T(8,128)S(1)}, u32[]{:S(2)}, u32[]{:S(2)}) collective-permute-start(f32[32,128]{1,0:T(8,128)S(1)} %slice.9), channel_id=1, source_target_pairs={{0,64},{32,96},{64,0},{96,32},{1,65},{33,97},{65,1},{97,33},{2,66}... | collective-permute-start | bytes 49160 | tf_op jit(solution)/shard_map/ppermute | solution.py:328
  27.7 2.2 %collective-permute-done.2 = f32[32,128]{1,0:T(8,128)S(1)} collective-permute-done((f32[32,128]{1,0:T(8,128)S(1)}, f32[32,128]{1,0:T(8,128)S(1)}, u32[]{:S(2)}, u32[]{:S(2)}) %collective-permute-start.2) | collective-permute-done | bytes 16416 | tf_op jit(solution)/shard_map/ppermute | solution.py:328
  29.9 0.6 %fusion = f32[1,32,128]{2,1,0:T(8,128)} fusion(f32[32,128]{1,0:T(8,128)S(1)} %collective-permute-done.2, f32[64,128]{1,0:T(8,128)S(1)} %add.6), kind=kLoop, calls=%fused_computation.1 | loop fusion | flops 4096 | bytes 49152 | tf_op jit(solution)/shard_map/broadcast_in_dim | solution.py:328
  (2 shorter events, 0.0 us)
Async XLA Ops:
  16.1 6.8 %collective-permute-start = (f32[256,128]{1,0:T(8,128)S(1)}, f32[256,128]{1,0:T(8,128)S(1)}, u32[]{:S(2)}, u32[]{:S(2)}) collective-permute-start(f32[256,128]{1,0:T(8,128)S(1)} %bitcast.4), channel_id=1, source_target_pairs={{0,1},{1,0},{2,3},{3,2},{4,5},{5,4},{6,7},{7,6},{8,9},{9,8},{10,11... | collective-permute-start | bytes 393224 | tf_op jit(solution)/shard_map/ppermute | solution.py:290
  24.7 1.3 %collective-permute-start.1 = (f32[64,128]{1,0:T(8,128)S(1)}, f32[64,128]{1,0:T(8,128)S(1)}, u32[]{:S(2)}, u32[]{:S(2)}) collective-permute-start(f32[64,128]{1,0:T(8,128)S(1)} %get-tuple-element.16), channel_id=1, source_target_pairs={{0,32},{32,0},{64,96},{96,64},{1,33},{33,1},{65,97},{97,65},{2,34}... | collective-permute-start | bytes 98312 | tf_op jit(solution)/shard_map/ppermute | solution.py:327
  26.0 3.8 %collective-permute-start.2 = (f32[32,128]{1,0:T(8,128)S(1)}, f32[32,128]{1,0:T(8,128)S(1)}, u32[]{:S(2)}, u32[]{:S(2)}) collective-permute-start(f32[32,128]{1,0:T(8,128)S(1)} %slice.9), channel_id=1, source_target_pairs={{0,64},{32,96},{64,0},{96,32},{1,65},{33,97},{65,1},{97,33},{2,66}... | collective-permute-start | bytes 49160 | tf_op jit(solution)/shard_map/ppermute | solution.py:328

commit v10 on v9

--- a/solution.py
+++ b/solution.py
@@ -19,12 +19,14 @@
     rows = lax.broadcasted_iota(jnp.int32, (LANES, LANES), 0)
     columns = lax.broadcasted_iota(jnp.int32, (LANES, LANES), 1)
     earlier = (rows < columns).astype(jnp.bfloat16)
-    running = jnp.zeros((flags.shape[0], 1), jnp.float32)
+    count = flags.shape[0]
+    pieces = [flags[:, start : start + LANES] for start in range(0, flags.shape[1], LANES)]
+    stacked = jnp.concatenate(pieces, axis=0)
+    inside = jnp.dot(stacked.astype(jnp.bfloat16), earlier, preferred_element_type=jnp.float32)
+    running = jnp.zeros((count, 1), jnp.float32)
     parts = []
-    for start in range(0, flags.shape[1], LANES):
-        piece = flags[:, start : start + LANES]
-        inside = jnp.dot(piece.astype(jnp.bfloat16), earlier, preferred_element_type=jnp.float32)
-        parts.append(inside + running)
+    for index, piece in enumerate(pieces):
+        parts.append(inside[index * count : (index + 1) * count] + running)
         running = running + jnp.sum(piece, axis=1, keepdims=True)
     return jnp.concatenate(parts, axis=1)
 

time: 30.7 us -> 30.6 us (level)
  no operation moved by 1% of the time
where the time goes in v10:
time: 30.6 us; the launch traced here: 30.5 us
  blocking collectives  14.9 us (49%)
  starting transfers between devices  5.61 us (18%)
  Pallas kernels  5.45 us (18%)
  waiting for transfers between devices  3.81 us (12%)
  other arithmetic  0.61 us (2%)
    all_to_all x1, blocking collectives, body(): near = lax.all_to_all(packed, 'facet', 0, 0, axis_index_groups=groups)  14.9 us
    ppermute x1, starting transfers between devices, body(): far = lax.ppermute(near, 'facet', [(i, i ^ 1) for i in range(2 * plane)])  3.88 us
    pallas_call x1, Pallas kernels, body(): pl.pallas_call(first_kernel, out_shape=(image, image, jax.ShapeDtypeStruc...  2.49 us
    ppermute x1, waiting for transfers between devices, body(): lax.ppermute(half[32:], 'freq', [(i, i ^ 2) for i in range(4)])  2.17 us
    pallas_call x1, Pallas kernels, body(): pl.pallas_call(functools.partial(last_kernel, 2.0 / math.sqrt(total)), ou...  1.81 us
    ppermute x1, starting transfers between devices, body(): lax.ppermute(half[32:], 'freq', [(i, i ^ 2) for i in range(4)])  1.65 us
    ppermute x1, waiting for transfers between devices, body(): half = keep + lax.ppermute(send, 'freq', [(i, i ^ 1) for i in range(4)])  1.19 us
    pallas_call x1, Pallas kernels, body(): pl.pallas_call(pack_kernel, out_shape=jax.ShapeDtypeStruct((plane, 16, LA...  1.15 us
  transfers between devices with their start and end apart: 3, of which 3 were waited for; matrix products, arithmetic and copies ran while one was open for 0% of the time, Pallas kernels for 8%

profile of v10, /device:TPU:0, one launch (start us, length us, event | category | flops | bytes accessed | tf_op | source)
XLA Modules:
  0.0 30.5 jit_solution(6557861580465540838)
XLA Ops:
  0.0 1.1 %shard_map.73 = f32[16,16,128]{2,1,0:T(8,128)S(1)} custom-call(f32[2,2,512]{2,1,0:T(2,128)} %vis_in.1, f32[2,512]{1,0:T(2,128)} %weight_in.1, s32[2,2,512]{2,1,0:T(2,128)} %uv_in.1, s32[2,512]{1,0:T(2,128)} %flag_in.1), custom_call_target="tpu_custom_call" | custom-call | tf_op jit(solution)/shard_map/pallas_call | solution.py:276
  1.2 14.9 %all_to_all.5 = f32[16,16,128]{2,1,0:T(8,128)S(1)} all-to-all(f32[16,16,128]{2,1,0:T(8,128)S(1)} %shard_map.73), channel_id=1, replica_groups={{0,2,4,6,8,10,12,14,16,18,20,22,24,26,28,30},{1,3,5,7,9,11,13,15,17,19,..., dimensions={0} | all-to-all | bytes 262144 | tf_op jit(solution)/shard_map/all_to_all | solution.py:290
  16.1 3.9 %collective-permute-start = (f32[256,128]{1,0:T(8,128)S(1)}, f32[256,128]{1,0:T(8,128)S(1)}, u32[]{:S(2)}, u32[]{:S(2)}) collective-permute-start(f32[256,128]{1,0:T(8,128)S(1)} %bitcast.4), channel_id=1, source_target_pairs={{0,1},{1,0},{2,3},{3,2},{4,5},{5,4},{6,7},{7,6},{8,9},{9,8},{10,11... | collective-permute-start | bytes 393224 | tf_op jit(solution)/shard_map/ppermute | solution.py:292
  20.0 2.5 %shard_map.74 = (f32[64,128]{1,0:T(8,128)S(1)}, f32[64,128]{1,0:T(8,128)S(1)}, f32[64,128]{1,0:T(8,128)S(1)}, s32[16,128]{1,0:T(8,128)S(1)}) custom-call(s32[1,64]{1,0:T(1,128)} %bitcast.6, f32[1,64]{1,0:T(1,128)} %beam_in.1, s32[1,2]{1,0:T(1,128)} %facet_in.1, f32[256,128]{1,0:T(8,128)S(1)} %bitcast.5), custom_call_target="tpu_custom_call" | custom-call | flops 268435456 | bytes 262144 | tf_op jit(solution)/shard_map/pallas_call | solution.py:304
  22.5 0.4 %collective-permute-done.data_ref = f32[256,128]{1,0:T(8,128)S(1)} collective-permute-done((f32[256,128]{1,0:T(8,128)S(1)}, f32[256,128]{1,0:T(8,128)S(1)}, u32[]{:S(2)}, u32[]{:S(2)}) %collective-permute-start) | collective-permute-done | bytes 131104 | tf_op jit(solution)/shard_map/ppermute | solution.py:292
  22.9 1.8 %shard_map.75 = (f32[64,128]{1,0:T(8,128)S(1)}, f32[64,128]{1,0:T(8,128)S(1)}) custom-call(s32[16,128]{1,0:T(8,128)S(1)} %get-tuple-element.11.centre_ref, f32[64,128]{1,0:T(8,128)S(1)} %get-tuple-element.12.gain_ref, f32[256,128]{1,0:T(8,128)S(1)} %collective-permute-done.data_ref, f32[64,128]{1,0:T(8,128)S(1)} %get-tuple-element.13.even_ref, ...), custom_call_target="tpu_custom_call" | custom-call | flops 268435456 | bytes 262144 | tf_op jit(solution)/shard_map/pallas_call | solution.py:320
  24.7 0.1 collective-permute-start.1
  24.8 1.2 %collective-permute-done.1 = f32[64,128]{1,0:T(8,128)S(1)} collective-permute-done((f32[64,128]{1,0:T(8,128)S(1)}, f32[64,128]{1,0:T(8,128)S(1)}, u32[]{:S(2)}, u32[]{:S(2)}) %collective-permute-start.1) | collective-permute-done | bytes 32800 | tf_op jit(solution)/shard_map/ppermute | solution.py:329
  26.0 1.6 %collective-permute-start.2 = (f32[32,128]{1,0:T(8,128)S(1)}, f32[32,128]{1,0:T(8,128)S(1)}, u32[]{:S(2)}, u32[]{:S(2)}) collective-permute-start(f32[32,128]{1,0:T(8,128)S(1)} %slice.9), channel_id=1, source_target_pairs={{0,64},{32,96},{64,0},{96,32},{1,65},{33,97},{65,1},{97,33},{2,66}... | collective-permute-start | bytes 49160 | tf_op jit(solution)/shard_map/ppermute | solution.py:330
  27.7 2.2 %collective-permute-done.2 = f32[32,128]{1,0:T(8,128)S(1)} collective-permute-done((f32[32,128]{1,0:T(8,128)S(1)}, f32[32,128]{1,0:T(8,128)S(1)}, u32[]{:S(2)}, u32[]{:S(2)}) %collective-permute-start.2) | collective-permute-done | bytes 16416 | tf_op jit(solution)/shard_map/ppermute | solution.py:330
  29.8 0.6 %fusion = f32[1,32,128]{2,1,0:T(8,128)} fusion(f32[32,128]{1,0:T(8,128)S(1)} %collective-permute-done.2, f32[64,128]{1,0:T(8,128)S(1)} %add.6), kind=kLoop, calls=%fused_computation.1 | loop fusion | flops 4096 | bytes 49152 | tf_op jit(solution)/shard_map/broadcast_in_dim | solution.py:330
  (2 shorter events, 0.0 us)
Async XLA Ops:
  16.1 6.8 %collective-permute-start = (f32[256,128]{1,0:T(8,128)S(1)}, f32[256,128]{1,0:T(8,128)S(1)}, u32[]{:S(2)}, u32[]{:S(2)}) collective-permute-start(f32[256,128]{1,0:T(8,128)S(1)} %bitcast.4), channel_id=1, source_target_pairs={{0,1},{1,0},{2,3},{3,2},{4,5},{5,4},{6,7},{7,6},{8,9},{9,8},{10,11... | collective-permute-start | bytes 393224 | tf_op jit(solution)/shard_map/ppermute | solution.py:292
  24.7 1.3 %collective-permute-start.1 = (f32[64,128]{1,0:T(8,128)S(1)}, f32[64,128]{1,0:T(8,128)S(1)}, u32[]{:S(2)}, u32[]{:S(2)}) collective-permute-start(f32[64,128]{1,0:T(8,128)S(1)} %get-tuple-element.16), channel_id=1, source_target_pairs={{0,32},{32,0},{64,96},{96,64},{1,33},{33,1},{65,97},{97,65},{2,34}... | collective-permute-start | bytes 98312 | tf_op jit(solution)/shard_map/ppermute | solution.py:329
  26.0 3.8 %collective-permute-start.2 = (f32[32,128]{1,0:T(8,128)S(1)}, f32[32,128]{1,0:T(8,128)S(1)}, u32[]{:S(2)}, u32[]{:S(2)}) collective-permute-start(f32[32,128]{1,0:T(8,128)S(1)} %slice.9), channel_id=1, source_target_pairs={{0,64},{32,96},{64,0},{96,32},{1,65},{33,97},{65,1},{97,33},{2,66}... | collective-permute-start | bytes 49160 | tf_op jit(solution)/shard_map/ppermute | solution.py:330
